TPU v7x, 32 devices: a whole 2x2x4 slice. The times are simulated.
32 devices in a mesh: beam: 2 (over x), chan: 8 (over z, y), tm: 2 (over core).
Axes of the slice: x: 2, y: 2, z: 4, core: 2. Of those that a mesh axis runs over, the one named last changes fastest.
Arguments:
- filterbank: bfloat16 [4096, 4096], P(('beam', 'chan'), 'tm'), parts along dimension 0, may hold values from -2500 to 2500
- local_delays: int32 [2048, 64], P('chan'), may hold values from 0 to 63
- lower_rows: int32 [3, 512], P(None, 'chan'), may hold values from 0 to 63
- upper_rows: int32 [3, 512], P(None, 'chan'), may hold values from 0 to 63
- level_shifts: int32 [3, 512], P(None, 'chan'), may hold values from 0 to 127, as said below
- box_widths: int32 [8], replicated, may hold values from 1 to 128, as said below
Outputs:
- snr: float32 [8, 1024, 4096], P(None, ('beam', 'chan'), 'tm'), parts along dimension 1
There are 2 independent parts, one for each index of `beam`. A program takes and returns all parts, laid end to end along the dimension named above; an argument that names none is the same for every part. Nothing has to cross between parts.
Inputs may be any that keep to these rules, and one draw needn't show every extreme that they name: `level_shifts`: at level j every entry is below 64 * 2**j // 2, and that bound less one occurs at every level. `box_widths`: entry i lies in [2**i, 2**(i+1)) for i below 7; the last entry is 128.
All inputs are finite; a program needn't handle non-finite values.
Results may differ from a plain program's by a relative error of at most 0.0014.
Values may be sent and summed in bfloat16 or wider, within the bound.
A program may use at most 64 MiB of HBM per device.

v0:
```python
import jax
import jax.numpy as jnp
from jax import lax
from jax.sharding import PartitionSpec as P

DLOC = 64


def shifted(block, axis, distance):
    devices = range(lax.axis_size(axis))
    route = [(i - distance, i) for i in devices if i - distance in devices]
    return lax.ppermute(block, axis, route)


def from_partner(array, axis, distance):
    return lax.ppermute(array, axis, [(i, i ^ 1 << distance) for i in range(lax.axis_size(axis))])


def for_sending(array):

    def short(part):
        return part.astype(jnp.bfloat16) if part.dtype == jnp.float32 else part

    return jax.tree.map(short, array)


def delay_rows(series, shift_by, start_at, length):
    current = series
    bit_count = max(start_at - 1, 0).bit_length()
    for bit_number in range(bit_count):
        amount = 2**bit_number
        moved = jnp.concatenate(
            [
                jnp.zeros((current.shape[0], amount), current.dtype),
                current[:, : current.shape[1] - amount],
            ],
            axis=1,
        )
        chosen = shift_by >> bit_number & 1 == 1
        current = jnp.where(chosen[:, None], moved, current)
    return current[:, start_at : start_at + length]


def dedisperse_local(filterbank, local_delays):
    samples = filterbank.shape[1]
    row_count = local_delays.shape[1]
    left_rim = shifted(filterbank[:, samples - (DLOC - 1) :], "tm", 1)
    extended = jnp.concatenate([left_rim, filterbank], axis=1)
    delays_by_row = local_delays.T
    group_size = min(16, DLOC)
    summed = jnp.zeros((row_count, samples), jnp.float32)
    for first_delay in range(0, DLOC, group_size):
        values_now = jnp.arange(first_delay, first_delay + group_size, dtype=jnp.int32)
        onehot = (delays_by_row[None, :, :] == values_now[:, None, None]).astype(jnp.bfloat16)
        products = jnp.einsum("gkc,ct->gkt", onehot, extended, preferred_element_type=jnp.float32)
        for offset in range(group_size):
            start_at = DLOC - 1 - (first_delay + offset)
            summed = summed + products[offset, :, start_at : start_at + samples]
    return summed


def merge_level(own_rows, level, lower_rows, upper_rows, level_shifts, reach_now):
    partner = from_partner(own_rows, "chan", level)
    upper_side = lax.axis_index("chan") >> level & 1 == 1
    lower_source = jnp.where(upper_side, partner, own_rows)[:, reach_now:]
    upper_source = jnp.where(upper_side, own_rows, partner)
    picked_low = jnp.take(lower_source, lower_rows[level], axis=0)
    picked_high = jnp.take(upper_source, upper_rows[level], axis=0)
    return picked_low + delay_rows(
        picked_high, level_shifts[level], reach_now, lower_source.shape[1]
    )


def local(filterbank, local_delays, lower_rows, upper_rows, level_shifts, box_widths):
    samples = filterbank.shape[1]
    dm_rows = dedisperse_local(filterbank, local_delays)
    row_count = dm_rows.shape[0]
    levels = lax.axis_size("chan").bit_length() - 1
    for level in range(levels):
        reach_now = DLOC * 2**level // 2
        left_rim = shifted(for_sending(dm_rows[:, samples - reach_now :]), "tm", 1)
        extended = jnp.concatenate([left_rim, dm_rows], axis=1)
        dm_rows = merge_level(extended, level, lower_rows, upper_rows, level_shifts, reach_now)
    square_sum = lax.psum(jnp.sum(dm_rows * dm_rows, axis=1), "tm")
    inverse_rms = lax.rsqrt(square_sum / (samples * lax.axis_size("tm")) + 1e-05)
    widest = 2 ** (box_widths.shape[0] - 1)
    tile_size = 128
    box_left = shifted(dm_rows[:, samples - (widest - 1) :], "tm", 1)
    padded = jnp.concatenate(
        [jnp.zeros((row_count, tile_size - widest + 1), jnp.float32), box_left, dm_rows], axis=1
    )
    tiles = samples // tile_size
    previous = padded[:, :samples].reshape(row_count, tiles, tile_size)
    current = padded[:, tile_size:].reshape(row_count, tiles, tile_size)
    rows_at = lax.broadcasted_iota(jnp.int32, (tile_size, tile_size), 0)[None, :, :]
    cols_at = lax.broadcasted_iota(jnp.int32, (tile_size, tile_size), 1)[None, :, :]
    reach_in = box_widths[:, None, None]
    current_mask = ((rows_at <= cols_at) & (rows_at > cols_at - reach_in)).astype(jnp.float32)
    previous_mask = (rows_at - tile_size > cols_at - reach_in).astype(jnp.float32)
    boxes = jnp.einsum(
        "kbu,wut->wkbt",
        previous,
        previous_mask,
        precision=lax.Precision.HIGHEST,
        preferred_element_type=jnp.float32,
    )
    boxes = boxes + jnp.einsum(
        "kbu,wut->wkbt",
        current,
        current_mask,
        precision=lax.Precision.HIGHEST,
        preferred_element_type=jnp.float32,
    )
    boxes = boxes.reshape(box_widths.shape[0], row_count, samples)
    return (
        boxes * inverse_rms[None, :, None] / jnp.sqrt(box_widths.astype(jnp.float32))[:, None, None]
    )


def solution(mesh):
    placed = (
        P(("beam", "chan"), "tm"),
        P("chan", None),
        P(None, "chan"),
        P(None, "chan"),
        P(None, "chan"),
        P(),
    )
    return jax.shard_map(
        local,
        mesh=mesh,
        in_specs=placed,
        out_specs=P(None, ("beam", "chan"), "tm"),
        check_vma=False,
    )
```

profile of v0, /device:TPU:0, one launch (start us, length us, event | category | flops | bytes accessed | tf_op | source)
XLA Modules:
  0.0 118.0 jit_solution(9590123697206058755)
XLA Ops:
  0.0 1.5 %copy.10 = bf16[256,2048]{0,1:T(8,128)(2,1)S(1)} copy(bf16[256,2048]{1,0:T(8,128)(2,1)} %param.8) | data formatting | bytes 2097152 | tf_op args[0]
  1.5 2.4 %collective-permute-start = (bf16[256,63]{0,1:T(8,128)(2,1)S(1)}, bf16[256,63]{0,1:T(8,128)(2,1)S(1)}, u32[]{:S(2)}, u32[]{:S(2)}) collective-permute-start(bf16[256,63]{0,1:T(8,128)(2,1)S(1)} %slice.427), channel_id=1, source_target_pairs={{0,1},{2,3},{4,5},{6,7},{8,9},{10,11},{12,13},{14,15},{16,17},{18,... | collective-permute-start | bytes 96776 | tf_op jit(solution)/shard_map/ppermute | solution.py:12
  4.8 1.5 %fusion.1 = f32[16,64,2111]{2,1,0:T(8,128)S(1)} fusion(s32[64,256]{1,0:T(8,128)S(1)} %bitcast.427, bf16[256,2048]{0,1:T(8,128)(2,1)S(1)} %copy.10, bf16[256,63]{0,1:T(8,128)(2,1)S(1)} %collective-permute-done), kind=kOutput, calls=%fused_computation.11 | convolution fusion | flops 1109195776 | bytes 9793024 | tf_op jit(solution)/shard_map/gkc,ct->gkt/dot_general | solution.py:55
  6.2 1.5 %fusion.4 = f32[16,64,2111]{2,1,0:T(8,128)S(1)} fusion(s32[64,256]{1,0:T(8,128)S(1)} %bitcast.428, s32[16]{0:T(128)S(1)} %iota_add_fusion.2, bf16[256,2048]{0,1:T(8,128)(2,1)S(1)} %copy.10, bf16[256,63]{0,1:T(8,128)(2,1)S(1)} %collective-permute-done), kind=kOutput, calls=%fused_computation.14 | convolution fusion | flops 1109195776 | bytes 9793088 | tf_op jit(solution)/shard_map/gkc,ct->gkt/dot_general | solution.py:55
  7.7 4.9 %fusion.6 = f32[16,64,2111]{2,1,0:T(8,128)} fusion(s32[64,256]{1,0:T(8,128)S(1)} %bitcast.429, s32[16]{0:T(128)S(1)} %iota_add_fusion.3, bf16[256,2048]{0,1:T(8,128)(2,1)S(1)} %copy.10, bf16[256,63]{0,1:T(8,128)(2,1)S(1)} %collective-permute-done), kind=kOutput, calls=%fused_computation.16 | convolution fusion | flops 1109195776 | bytes 9793088 | tf_op jit(solution)/shard_map/gkc,ct->gkt/dot_general | solution.py:55
  12.6 4.9 %fusion.2 = f32[16,64,2111]{2,1,0:T(8,128)} fusion(s32[64,256]{1,0:T(8,128)S(1)} %bitcast.430, s32[16]{0:T(128)S(1)} %iota_add_fusion.1, bf16[256,2048]{0,1:T(8,128)(2,1)S(1)} %copy.10, bf16[256,63]{0,1:T(8,128)(2,1)S(1)} %collective-permute-done), kind=kOutput, calls=%fused_computation.12 | convolution fusion | flops 1109195776 | bytes 9793088 | tf_op jit(solution)/shard_map/gkc,ct->gkt/dot_general | solution.py:55
  17.5 12.3 %fusion.20 = f32[64,2048]{1,0:T(8,128)S(1)} fusion(f32[16,64,2111]{2,1,0:T(8,128)} %fusion.2, f32[16,64,2111]{2,1,0:T(8,128)S(1)} %fusion.4, f32[16,64,2111]{2,1,0:T(8,128)} %fusion.6, f32[16,64,2111]{2,1,0:T(8,128)S(1)} %fusion.1), kind=kLoop, calls=%fused_computation.61 | loop fusion | flops 8257536 | bytes 34078720 | tf_op jit(solution)/shard_map/add | solution.py:58
  30.0 2.4 %collective-permute-start.1 = (bf16[64,32]{1,0:T(8,128)(2,1)S(1)}, bf16[64,32]{1,0:T(8,128)(2,1)S(1)}, u32[]{:S(2)}, u32[]{:S(2)}) collective-permute-start(bf16[64,32]{1,0:T(8,128)(2,1)S(1)} %slice.880), channel_id=1, source_target_pairs={{0,1},{2,3},{4,5},{6,7},{8,9},{10,11},{12,13},{14,15},{16,17},{18,... | collective-permute-start | bytes 12296 | tf_op jit(solution)/shard_map/ppermute | solution.py:12
  33.3 2.4 %collective-permute-start.2 = (f32[64,2080]{1,0:T(8,128)S(1)}, f32[64,2080]{1,0:T(8,128)S(1)}, u32[]{:S(2)}, u32[]{:S(2)}) collective-permute-start(f32[64,2080]{1,0:T(8,128)S(1)} %pad_maximum_fusion), channel_id=1, source_target_pairs={{0,2},{2,0},{4,6},{6,4},{8,10},{10,8},{12,14},{14,12},{1,3},{3,1},... | collective-permute-start | bytes 1597448 | tf_op jit(solution)/shard_map/ppermute | solution.py:16
  35.7 13.1 %collective-permute-done.2 = f32[64,2080]{1,0:T(8,128)S(1)} collective-permute-done((f32[64,2080]{1,0:T(8,128)S(1)}, f32[64,2080]{1,0:T(8,128)S(1)}, u32[]{:S(2)}, u32[]{:S(2)}) %collective-permute-start.2) | collective-permute-done | bytes 532512 | tf_op jit(solution)/shard_map/ppermute | solution.py:16
  52.3 1.7 %collective-permute-start.3 = (bf16[64,64]{1,0:T(8,128)(2,1)S(1)}, bf16[64,64]{1,0:T(8,128)(2,1)S(1)}, u32[]{:S(2)}, u32[]{:S(2)}) collective-permute-start(bf16[64,64]{1,0:T(8,128)(2,1)S(1)} %slice.879), channel_id=1, source_target_pairs={{0,1},{2,3},{4,5},{6,7},{8,9},{10,11},{12,13},{14,15},{16,17},{18,... | collective-permute-start | bytes 24584 | tf_op jit(solution)/shard_map/ppermute | solution.py:12
  53.9 0.8 collective-permute-done.3
  55.0 1.6 %collective-permute-start.4 = (f32[64,2112]{1,0:T(8,128)S(1)}, f32[64,2112]{1,0:T(8,128)S(1)}, u32[]{:S(2)}, u32[]{:S(2)}) collective-permute-start(f32[64,2112]{1,0:T(8,128)S(1)} %pad_maximum_fusion.1), channel_id=1, source_target_pairs={{0,4},{2,6},{4,0},{6,2},{8,12},{10,14},{12,8},{14,10},{1,5},{3,7},... | collective-permute-start | bytes 1622024 | tf_op jit(solution)/shard_map/ppermute | solution.py:16
  56.6 13.3 %collective-permute-done.4 = f32[64,2112]{1,0:T(8,128)S(1)} collective-permute-done((f32[64,2112]{1,0:T(8,128)S(1)}, f32[64,2112]{1,0:T(8,128)S(1)}, u32[]{:S(2)}, u32[]{:S(2)}) %collective-permute-start.4) | collective-permute-done | bytes 540704 | tf_op jit(solution)/shard_map/ppermute | solution.py:16
  73.5 1.4 %collective-permute-start.5 = (bf16[64,128]{1,0:T(8,128)(2,1)S(1)}, bf16[64,128]{1,0:T(8,128)(2,1)S(1)}, u32[]{:S(2)}, u32[]{:S(2)}) collective-permute-start(bf16[64,128]{1,0:T(8,128)(2,1)S(1)} %slice.878), channel_id=1, source_target_pairs={{0,1},{2,3},{4,5},{6,7},{8,9},{10,11},{12,13},{14,15},{16,17},{18,... | collective-permute-start | bytes 49160 | tf_op jit(solution)/shard_map/ppermute | solution.py:12
  75.0 0.8 collective-permute-done.5
  75.9 2.7 %collective-permute-start.6 = (f32[64,2176]{1,0:T(8,128)S(1)}, f32[64,2176]{1,0:T(8,128)S(1)}, u32[]{:S(2)}, u32[]{:S(2)}) collective-permute-start(f32[64,2176]{1,0:T(8,128)S(1)} %pad_maximum_fusion.2), channel_id=1, source_target_pairs={{0,8},{2,10},{4,12},{6,14},{8,0},{10,2},{12,4},{14,6},{1,9},{3,11}... | collective-permute-start | bytes 1671176 | tf_op jit(solution)/shard_map/ppermute | solution.py:16
  78.6 25.1 %collective-permute-done.6 = f32[64,2176]{1,0:T(8,128)S(1)} collective-permute-done((f32[64,2176]{1,0:T(8,128)S(1)}, f32[64,2176]{1,0:T(8,128)S(1)}, u32[]{:S(2)}, u32[]{:S(2)}) %collective-permute-start.6) | collective-permute-done | bytes 557088 | tf_op jit(solution)/shard_map/ppermute | solution.py:16
  104.5 0.8 gather_fusion.2
  107.2 1.4 %collective-permute-start.7 = (f32[64,127]{1,0:T(8,128)S(1)}, f32[64,127]{1,0:T(8,128)S(1)}, u32[]{:S(2)}, u32[]{:S(2)}) collective-permute-start(f32[64,127]{1,0:T(8,128)S(1)} %slice.525), channel_id=1, source_target_pairs={{0,1},{2,3},{4,5},{6,7},{8,9},{10,11},{12,13},{14,15},{16,17},{18,... | collective-permute-start | bytes 97544 | tf_op jit(solution)/shard_map/ppermute | solution.py:12
  108.6 2.5 %psum.7 = f32[64]{0:T(128)S(1)} all-reduce(f32[64]{0:T(128)S(1)} %get-tuple-element.6), channel_id=1, replica_groups=mesh['beam'=2,'chan'=8,'tm'=2] {'tm'}, use_global_device_ids=true, to_apply=%region_1.3 | all-reduce | flops 64 | bytes 512 | tf_op jit(solution)/shard_map/psum | solution.py:84
  111.2 1.9 %fusion.15 = f32[8,128,64,16]{1,2,3,0:T(8,128)S(1)} fusion(s32[8]{0:T(128)S(1)} %copy-done.2, s32[128,128]{1,0:T(8,128)S(1)} %iota_add_fusion, f32[64,2176]{1,0:T(8,128)S(1)} %concatenate.91), kind=kOutput, calls=%fused_computation.51 | convolution fusion | flops 1610874880 | bytes 4784640 | tf_op jit(solution)/shard_map/kbu,wut->wkbt/dot_general | solution.py:100
  113.2 2.2 %add_bitcast_fusion = f32[8,16,8,8,128]{4,3,2,1,0:T(8,128)S(1)} fusion(f32[8,128,64,16]{1,2,3,0:T(8,128)S(1)} %fusion.15, s32[8]{0:T(128)S(1)} %copy-done.2, pred[128,128]{1,0:T(8,128)(4,1)S(1)} %iota_compare_fusion.3, f32[64,2048]{1,0:T(8,128)S(1)} %get-tuple-element.7), kind=kOutput, calls=%fused_computation.8 | convolution fusion | flops 1612054528 | bytes 8929312 | tf_op jit(solution)/shard_map/kbu,wut->wkbt/dot_general | solution.py:107
  115.3 2.7 %fusion = f32[8,64,2048]{2,1,0:T(8,128)} fusion(f32[8,16,8,8,128]{4,3,2,1,0:T(8,128)S(1)} %add_bitcast_fusion, f32[8]{0:T(128)S(1)} %convert_sqrt_fusion, f32[64]{0:T(128)S(1)} %add_rsqrt_fusion), kind=kLoop, calls=%fused_computation.7 | loop fusion | flops 2097152 | bytes 8388896 | tf_op jit(solution)/shard_map/div | solution.py:116
  (75 shorter events, 11.8 us)
Async XLA Ops:
  0.0 3.9 %copy-start.3 = (s32[3,64]{1,0:T(4,128)S(1)}, s32[3,64]{1,0:T(4,128)}, u32[]{:S(2)}) copy-start(s32[3,64]{1,0:T(4,128)} %param.10) | copy-start | bytes 2308
  0.0 4.0 %copy-start.1 = (s32[3,64]{1,0:T(4,128)S(1)}, s32[3,64]{1,0:T(4,128)}, u32[]{:S(2)}) copy-start(s32[3,64]{1,0:T(4,128)} %param.11) | copy-start | bytes 2308
  0.0 4.8 %copy-start = (s32[256,64]{0,1:T(8,128)S(1)}, s32[256,64]{0,1:T(8,128)}, u32[]{:S(2)}) copy-start(s32[256,64]{0,1:T(8,128)} %param.9) | copy-start | bytes 196612
  1.5 3.2 %collective-permute-start = (bf16[256,63]{0,1:T(8,128)(2,1)S(1)}, bf16[256,63]{0,1:T(8,128)(2,1)S(1)}, u32[]{:S(2)}, u32[]{:S(2)}) collective-permute-start(bf16[256,63]{0,1:T(8,128)(2,1)S(1)} %slice.427), channel_id=1, source_target_pairs={{0,1},{2,3},{4,5},{6,7},{8,9},{10,11},{12,13},{14,15},{16,17},{18,... | collective-permute-start | bytes 96776 | tf_op jit(solution)/shard_map/ppermute | solution.py:12
  17.5 18.1 %copy-start.4 = (s32[3,64]{1,0:T(4,128)S(1)}, s32[3,64]{1,0:T(4,128)}, u32[]{:S(2)}) copy-start(s32[3,64]{1,0:T(4,128)} %param.12) | copy-start | bytes 2308
  30.0 3.1 %collective-permute-start.1 = (bf16[64,32]{1,0:T(8,128)(2,1)S(1)}, bf16[64,32]{1,0:T(8,128)(2,1)S(1)}, u32[]{:S(2)}, u32[]{:S(2)}) collective-permute-start(bf16[64,32]{1,0:T(8,128)(2,1)S(1)} %slice.880), channel_id=1, source_target_pairs={{0,1},{2,3},{4,5},{6,7},{8,9},{10,11},{12,13},{14,15},{16,17},{18,... | collective-permute-start | bytes 12296 | tf_op jit(solution)/shard_map/ppermute | solution.py:12
  33.3 15.5 %collective-permute-start.2 = (f32[64,2080]{1,0:T(8,128)S(1)}, f32[64,2080]{1,0:T(8,128)S(1)}, u32[]{:S(2)}, u32[]{:S(2)}) collective-permute-start(f32[64,2080]{1,0:T(8,128)S(1)} %pad_maximum_fusion), channel_id=1, source_target_pairs={{0,2},{2,0},{4,6},{6,4},{8,10},{10,8},{12,14},{14,12},{1,3},{3,1},... | collective-permute-start | bytes 1597448 | tf_op jit(solution)/shard_map/ppermute | solution.py:16
  52.3 2.5 %collective-permute-start.3 = (bf16[64,64]{1,0:T(8,128)(2,1)S(1)}, bf16[64,64]{1,0:T(8,128)(2,1)S(1)}, u32[]{:S(2)}, u32[]{:S(2)}) collective-permute-start(bf16[64,64]{1,0:T(8,128)(2,1)S(1)} %slice.879), channel_id=1, source_target_pairs={{0,1},{2,3},{4,5},{6,7},{8,9},{10,11},{12,13},{14,15},{16,17},{18,... | collective-permute-start | bytes 24584 | tf_op jit(solution)/shard_map/ppermute | solution.py:12
  55.0 14.9 %collective-permute-start.4 = (f32[64,2112]{1,0:T(8,128)S(1)}, f32[64,2112]{1,0:T(8,128)S(1)}, u32[]{:S(2)}, u32[]{:S(2)}) collective-permute-start(f32[64,2112]{1,0:T(8,128)S(1)} %pad_maximum_fusion.1), channel_id=1, source_target_pairs={{0,4},{2,6},{4,0},{6,2},{8,12},{10,14},{12,8},{14,10},{1,5},{3,7},... | collective-permute-start | bytes 1622024 | tf_op jit(solution)/shard_map/ppermute | solution.py:16
  72.9 5.6 %copy-start.2 = (s32[8]{0:T(128)S(1)}, s32[8]{0:T(128)}, u32[]{:S(2)}) copy-start(s32[8]{0:T(128)} %param.13) | copy-start | bytes 100
  73.5 2.3 %collective-permute-start.5 = (bf16[64,128]{1,0:T(8,128)(2,1)S(1)}, bf16[64,128]{1,0:T(8,128)(2,1)S(1)}, u32[]{:S(2)}, u32[]{:S(2)}) collective-permute-start(bf16[64,128]{1,0:T(8,128)(2,1)S(1)} %slice.878), channel_id=1, source_target_pairs={{0,1},{2,3},{4,5},{6,7},{8,9},{10,11},{12,13},{14,15},{16,17},{18,... | collective-permute-start | bytes 49160 | tf_op jit(solution)/shard_map/ppermute | solution.py:12
  75.9 27.8 %collective-permute-start.6 = (f32[64,2176]{1,0:T(8,128)S(1)}, f32[64,2176]{1,0:T(8,128)S(1)}, u32[]{:S(2)}, u32[]{:S(2)}) collective-permute-start(f32[64,2176]{1,0:T(8,128)S(1)} %pad_maximum_fusion.2), channel_id=1, source_target_pairs={{0,8},{2,10},{4,12},{6,14},{8,0},{10,2},{12,4},{14,6},{1,9},{3,11}... | collective-permute-start | bytes 1671176 | tf_op jit(solution)/shard_map/ppermute | solution.py:16
  107.2 3.9 %collective-permute-start.7 = (f32[64,127]{1,0:T(8,128)S(1)}, f32[64,127]{1,0:T(8,128)S(1)}, u32[]{:S(2)}, u32[]{:S(2)}) collective-permute-start(f32[64,127]{1,0:T(8,128)S(1)} %slice.525), channel_id=1, source_target_pairs={{0,1},{2,3},{4,5},{6,7},{8,9},{10,11},{12,13},{14,15},{16,17},{18,... | collective-permute-start | bytes 97544 | tf_op jit(solution)/shard_map/ppermute | solution.py:12
where the time goes:
time: 118 us
  waiting for transfers between devices  54.4 us (46%)
  other arithmetic  21.3 us (18%)
  matrix products  16.9 us (14%)
  starting transfers between devices  16.1 us (14%)
  local copies, waits for them, and re-layouts  6.52 us (6%)
  blocking collectives  2.47 us (2%)
    ppermute x3, waiting for transfers between devices, from_partner(): lax.ppermute(array, axis, [(i, i ^ 1 << distance) for i in range(lax.axis...  51.4 us
    dot_general x4, matrix products, dedisperse_local(): jnp.einsum('gkc,ct->gkt', onehot, extended, preferred_element_type=jnp.fl...  12.8 us
    add x1, other arithmetic, dedisperse_local(): summed = summed + products[offset, :, start_at:start_at + samples]  12.3 us
    ppermute x5, starting transfers between devices, shifted(): return lax.ppermute(block, axis, route)  9.36 us
    ppermute x3, starting transfers between devices, from_partner(): lax.ppermute(array, axis, [(i, i ^ 1 << distance) for i in range(lax.axis...  6.7 us
    select_n x15, other arithmetic, delay_rows(): current = jnp.where(chosen[:, None], moved, current)  3.31 us
    ppermute x5, waiting for transfers between devices, shifted(): return lax.ppermute(block, axis, route)  3 us
    div x1, other arithmetic, local(): boxes * inverse_rms[None, :, None]  2.68 us
  transfers between devices with their start and end apart: 8, of which 7 were waited for; matrix products, arithmetic and copies ran while one was open for 0% of the time, Pallas kernels for 0%

commit v1 on v0

v1 whole, which is shorter than its diff:
```python
import functools

import jax
import jax.numpy as jnp
from jax import lax
from jax.experimental import pallas as pl
from jax.experimental.pallas import tpu as pltpu
from jax.sharding import PartitionSpec as P

DLOC = 64
LANES = 128
FINE = 8
COARSE = DLOC // FINE


def lane_up(count):
    return -(-count // LANES) * LANES


def from_earlier(block, axis, distance):
    devices = range(lax.axis_size(axis))
    route = [(i - distance, i) for i in devices if i - distance in devices]
    return lax.ppermute(block, axis, route)


def from_partner(array, axis, distance):
    return lax.ppermute(array, axis, [(i, i ^ 1 << distance) for i in range(lax.axis_size(axis))])


def left_context(block, axis, width):
    samples = block.shape[1]
    pieces = []
    distance = 1
    while width > 0:
        part = min(width, samples)
        if distance < lax.axis_size(axis):
            pieces.insert(0, from_earlier(block[:, samples - part :], axis, distance))
        else:
            pieces.insert(0, jnp.zeros((block.shape[0], width), block.dtype))
            part = width
        width -= part
        distance += 1
    return pieces[0] if len(pieces) == 1 else jnp.concatenate(pieces, axis=1)


def code_rows(rows):
    largest = jnp.maximum(jnp.max(jnp.abs(rows), axis=1, keepdims=True), 2.0**-100)
    exponent = jnp.floor(jnp.log2(largest))
    coded = jnp.round(jnp.clip(rows * jnp.exp2(14.0 - exponent), -32767.0, 32767.0))
    column = lax.broadcasted_iota(jnp.int32, rows.shape, 1)
    return jnp.where(column == 0, exponent, coded).astype(jnp.int32).astype(jnp.int16)


def decode_rows(coded):
    values = coded.astype(jnp.int32).astype(jnp.float32)
    return values * jnp.exp2(values[:, :1] - 14.0)


def dedisperse_kernel(tile, rim_ref, fb_ref, delays_ref, own_ref, coded_ref, ext, onehot, spread, partial):
    channels, samples = fb_ref.shape
    rows = delays_ref.shape[0]
    rim = rim_ref.shape[1]
    total = rim + samples
    ext[:, :LANES] = jnp.zeros((channels, LANES), jnp.bfloat16)
    ext[:, LANES : LANES + rim] = rim_ref[...]
    ext[:, LANES + rim :] = fb_ref[...]
    for coarse in range(COARSE):
        relative = delays_ref[...] - FINE * coarse
        for fine in range(FINE):
            onehot[coarse * rows : (coarse + 1) * rows, fine * channels : (fine + 1) * channels] = (
                jnp.where(relative == fine, 1.0, 0.0).astype(jnp.bfloat16)
            )

    def step(index, carry):
        start = pl.multiple_of(index * tile, LANES)
        window = ext[:, pl.ds(start, tile + LANES)]
        for fine in range(FINE):
            spread[fine * channels : (fine + 1) * channels, :] = window[
                :, LANES - fine : LANES - fine + tile
            ]
        partial[:, pl.ds(start, tile)] = jnp.dot(
            onehot[...], spread[...], preferred_element_type=jnp.float32
        )
        return carry

    lax.fori_loop(0, total // tile, step, 0)
    width = own_ref.shape[1]
    summed = partial[:rows, total - width :]
    for coarse in range(1, COARSE):
        back = total - width - FINE * coarse
        summed = summed + partial[coarse * rows : (coarse + 1) * rows, back : back + width]
    own_ref[...] = summed
    coded_ref[...] = code_rows(summed)


def dedisperse(rim, filterbank, delays, width):
    channels, samples = filterbank.shape
    rows = delays.shape[0]
    total = rim.shape[1] + samples
    tile = max(t for t in (512, 256, 128) if total % t == 0)
    return pl.pallas_call(
        functools.partial(dedisperse_kernel, tile),
        name="dedisperse",
        out_shape=(
            jax.ShapeDtypeStruct((rows, width), jnp.float32),
            jax.ShapeDtypeStruct((rows, width), jnp.int16),
        ),
        scratch_shapes=[
            pltpu.VMEM((channels, LANES + total), jnp.bfloat16),
            pltpu.VMEM((COARSE * rows, FINE * channels), jnp.bfloat16),
            pltpu.VMEM((FINE * channels, tile), jnp.bfloat16),
            pltpu.VMEM((COARSE * rows, total), jnp.float32),
        ],
        compiler_params=pltpu.CompilerParams(vmem_limit_bytes=40 * 2**20),
    )(rim, filterbank, delays)


def pick(index, source):
    rows = source.shape[0]
    chosen = jnp.where(
        lax.broadcasted_iota(jnp.int32, (index.shape[0], 2 * rows), 1) % rows == index, 1.0, 0.0
    ).astype(jnp.bfloat16)
    high = source.astype(jnp.bfloat16)
    low = (source - high.astype(jnp.float32)).astype(jnp.bfloat16)
    return jnp.dot(
        chosen, jnp.concatenate([high, low], axis=0), preferred_element_type=jnp.float32
    )


def merge_kernel(level, levels, side_ref, own_ref, coded_ref, plan_ref, *out_refs):
    reach = DLOC * 2**level // 2
    own = own_ref[...]
    partner = decode_rows(coded_ref[...])
    upper_side = side_ref[0] == 1
    low_source = jnp.where(upper_side, partner, own)
    high_source = jnp.where(upper_side, own, partner)
    plan = plan_ref[...]
    low = pick(plan[:, level : level + 1], low_source)
    high = pick(plan[:, levels + level : levels + level + 1], high_source)
    shift = plan[:, 2 * levels + level : 2 * levels + level + 1]
    for bit in range((reach - 1).bit_length()):
        high = jnp.where((shift >> bit) & 1 == 1, pltpu.roll(high, 2**bit, 1), high)
    column = lax.broadcasted_iota(jnp.int32, high.shape, 1)
    merged = low + jnp.where(column < shift, 0.0, high)
    width = out_refs[0].shape[1]
    merged = merged[:, merged.shape[1] - width :]
    out_refs[0][...] = merged
    if level < levels - 1:
        out_refs[1][...] = code_rows(merged)
    else:
        fresh = merged[:, LANES:]
        out_refs[1][...] = jnp.sum(fresh * fresh, axis=1, keepdims=True)


def merge(level, levels, side, own, coded, plan, width):
    rows = own.shape[0]
    second = (
        jax.ShapeDtypeStruct((rows, width), jnp.int16)
        if level < levels - 1
        else jax.ShapeDtypeStruct((rows, 1), jnp.float32)
    )
    vmem = pl.BlockSpec(memory_space=pltpu.VMEM)
    return pl.pallas_call(
        functools.partial(merge_kernel, level, levels),
        name=f"merge_{level}",
        out_shape=(jax.ShapeDtypeStruct((rows, width), jnp.float32), second),
        in_specs=[pl.BlockSpec(memory_space=pltpu.SMEM), vmem, vmem, vmem],
        out_specs=(vmem, vmem),
        compiler_params=pltpu.CompilerParams(vmem_limit_bytes=32 * 2**20),
    )(side, own, coded, plan)


def box_kernel(times, widths_ref, state_ref, squares_ref, out_ref, stacked):
    rows = state_ref.shape[0]
    tiles = out_ref.shape[2] // LANES
    per_step = out_ref.shape[0]

    @pl.when(pl.program_id(0) == 0)
    def _():
        for tile in range(tiles):
            part = state_ref[:, tile * LANES : (tile + 2) * LANES]
            high = part.astype(jnp.bfloat16)
            low = (part - high.astype(jnp.float32)).astype(jnp.bfloat16)
            stacked[tile * rows : (tile + 1) * rows, : 2 * LANES] = high
            stacked[tile * rows : (tile + 1) * rows, 2 * LANES :] = low

    inverse = lax.rsqrt(squares_ref[...] / times + 1e-05)
    masks = []
    factors = []
    for which in range(per_step):
        box_width = widths_ref[pl.program_id(0) * per_step + which]
        at = lax.broadcasted_iota(jnp.int32, (2 * LANES, LANES), 0) - LANES
        to = lax.broadcasted_iota(jnp.int32, (2 * LANES, LANES), 1)
        inside = (at <= to) & (at > to - box_width)
        mask = jnp.where(inside, 1.0, 0.0).astype(jnp.bfloat16)
        masks.append(jnp.concatenate([mask, mask], axis=0))
        root = jnp.sqrt(jnp.full((rows, LANES), box_width.astype(jnp.float32)))
        factors.append(inverse / root)
    boxes = jnp.dot(
        stacked[...], jnp.concatenate(masks, axis=1), preferred_element_type=jnp.float32
    )
    for which in range(per_step):
        for tile in range(tiles):
            out_ref[which, :, tile * LANES : (tile + 1) * LANES] = (
                boxes[tile * rows : (tile + 1) * rows, which * LANES : (which + 1) * LANES]
                * factors[which]
            )


def box_filter(widths, state, squares, samples, times):
    rows = state.shape[0]
    count = widths.shape[0]
    per_step = 2 if count % 2 == 0 else 1
    return pl.pallas_call(
        functools.partial(box_kernel, times),
        name="boxes",
        grid=(count // per_step,),
        out_shape=jax.ShapeDtypeStruct((count, rows, samples), jnp.float32),
        in_specs=[
            pl.BlockSpec(memory_space=pltpu.SMEM),
            pl.BlockSpec(memory_space=pltpu.VMEM),
            pl.BlockSpec(memory_space=pltpu.VMEM),
        ],
        out_specs=pl.BlockSpec((per_step, rows, samples), lambda i: (i, 0, 0)),
        scratch_shapes=[pltpu.VMEM((samples // LANES * rows, 4 * LANES), jnp.bfloat16)],
        compiler_params=pltpu.CompilerParams(vmem_limit_bytes=32 * 2**20),
    )(widths, state, squares)


def local(filterbank, local_delays, lower_rows, upper_rows, level_shifts, box_widths):
    samples = filterbank.shape[1]
    levels = lax.axis_size("chan").bit_length() - 1
    needs = [LANES]
    for level in reversed(range(levels)):
        needs.insert(0, needs[0] - (level == levels - 1) + DLOC * 2**level // 2 - 1)
    widths = [samples + lane_up(need + 1) for need in needs[:-1]] + [samples + LANES]
    rim = left_context(filterbank, "tm", lane_up(widths[0] - samples + DLOC - 1))
    plan = jnp.concatenate([lower_rows, upper_rows, level_shifts], axis=0).T
    own, coded = dedisperse(rim, filterbank, local_delays.T, widths[0])
    for level in range(levels):
        side = (lax.axis_index("chan") >> level & 1).astype(jnp.int32)[None]
        partner = from_partner(coded, "chan", level)
        own, coded = merge(level, levels, side, own, partner, plan, widths[level + 1])
    squares = lax.psum(coded, "tm")
    return box_filter(box_widths, own, squares, samples, samples * lax.axis_size("tm"))


def solution(mesh):
    placed = (
        P(("beam", "chan"), "tm"),
        P("chan", None),
        P(None, "chan"),
        P(None, "chan"),
        P(None, "chan"),
        P(),
    )
    return jax.shard_map(
        local,
        mesh=mesh,
        in_specs=placed,
        out_specs=P(None, ("beam", "chan"), "tm"),
        check_vma=False,
    )
```

time: 118 us -> 62.2 us (0.53)
  waiting for transfers between devices: 54.4 us -> 27.9 us
  other arithmetic: 21.3 us -> 0.72 us
  Pallas kernels: 0 us -> 17.4 us
  matrix products: 16.9 us -> 0 us
  starting transfers between devices: 16.1 us -> 9.3 us
  local copies, waits for them, and re-layouts: 6.52 us -> 3.14 us
    ppermute x3, waiting for transfers between devices: 51.4 us -> 26.8 us  [from_partner(): lax.ppermute(array, axis, [(i, i ^ 1 << distance) for i in range(lax.axis...]
    pallas_call x0 -> x5, Pallas kernels: none -> 17.4 us  [the longest x1 8.24 us: dedisperse(): pl.pallas_call(functools.partial(dedisperse_kernel, tile), name='dedisper...]
    dot_general x6 -> x0, matrix products: 16.9 us -> none  [the longest x4 12.8 us: dedisperse_local(): jnp.einsum('gkc,ct->gkt', onehot, extended, preferred_element_type=jnp.fl...]
    add x6 -> x0, other arithmetic: 13.1 us -> none  [the longest x1 12.3 us: dedisperse_local(): summed = summed + products[offset, :, start_at:start_at + samples]]
    ppermute x5 -> x1, starting transfers between devices: 9.36 us -> 2.37 us  [from_earlier(): return lax.ppermute(block, axis, route)]
    gather x6 -> x0, local copies, waits for them, and re-layouts: 4.66 us -> none  [the longest x3 2.39 us: merge_level(): picked_high = jnp.take(upper_source, upper_rows[level], axis=0)]
    select_n x25 -> x0, other arithmetic: 4.6 us -> none  [the longest x15 3.31 us: delay_rows(): current = jnp.where(chosen[:, None], moved, current)]
    div x1 -> x0, other arithmetic: 2.68 us -> none  [local(): boxes * inverse_rms[None, :, None]]
  transfers between devices with their start and end apart: 8 -> 4, of which waited for: 7 -> 4; matrix products, arithmetic and copies ran while one was open for 0% -> 1% of each run, Pallas kernels for 0% -> 0%
where the time goes in v1:
time: 62.2 us; the launch traced here: 62 us
  waiting for transfers between devices  27.9 us (45%)
  Pallas kernels  17.4 us (28%)
  starting transfers between devices  9.3 us (15%)
  blocking collectives  3.4 us (5%)
  local copies, waits for them, and re-layouts  3.14 us (5%)
  other arithmetic  0.72 us (1%)
    ppermute x3, waiting for transfers between devices, from_partner(): lax.ppermute(array, axis, [(i, i ^ 1 << distance) for i in range(lax.axis...  26.8 us
    pallas_call x1, Pallas kernels, dedisperse(): pl.pallas_call(functools.partial(dedisperse_kernel, tile), name='dedisper...  8.24 us
    ppermute x3, starting transfers between devices, from_partner(): lax.ppermute(array, axis, [(i, i ^ 1 << distance) for i in range(lax.axis...  6.93 us
    pallas_call x3, Pallas kernels, merge(): pl.pallas_call(functools.partial(merge_kernel, level, levels), name=f'mer...  5.24 us
    pallas_call x1, Pallas kernels, box_filter(): pl.pallas_call(functools.partial(box_kernel, times), name='boxes', grid=(...  3.94 us
    psum x1, blocking collectives, local(): squares = lax.psum(coded, 'tm')  3.4 us
    ppermute x1, starting transfers between devices, from_earlier(): return lax.ppermute(block, axis, route)  2.37 us
    unnamed x6, local copies, waits for them, and re-layouts  2.07 us
  transfers between devices with their start and end apart: 4, of which 4 were waited for; matrix products, arithmetic and copies ran while one was open for 1% of the time, Pallas kernels for 0%

profile of v1, /device:TPU:0, one launch (start us, length us, event | category | flops | bytes accessed | tf_op | source)
XLA Modules:
  0.0 62.0 jit_solution(13332553724541834741)
XLA Ops:
  0.0 0.0 copy-start.2
  0.0 1.0 %slice.3 = bf16[256,512]{1,0:T(8,128)(2,1)S(1)} slice(bf16[256,2048]{1,0:T(8,128)(2,1)} %fb_ref.1), slice={[0:256], [1536:2048]} | slice | bytes 524288 | tf_op jit(solution)/shard_map/slice | solution.py:37
  1.0 2.4 %collective-permute-start = (bf16[256,512]{1,0:T(8,128)(2,1)S(1)}, bf16[256,512]{1,0:T(8,128)(2,1)S(1)}, u32[]{:S(2)}, u32[]{:S(2)}) collective-permute-start(bf16[256,512]{1,0:T(8,128)(2,1)S(1)} %slice.3), channel_id=1, source_target_pairs={{0,1},{2,3},{4,5},{6,7},{8,9},{10,11},{12,13},{14,15},{16,17},{18,... | collective-permute-start | bytes 786440 | tf_op jit(solution)/shard_map/ppermute | solution.py:23
  3.4 1.1 %collective-permute-done.rim_ref = bf16[256,512]{1,0:T(8,128)(2,1)S(1)} collective-permute-done((bf16[256,512]{1,0:T(8,128)(2,1)S(1)}, bf16[256,512]{1,0:T(8,128)(2,1)S(1)}, u32[]{:S(2)}, u32[]{:S(2)}) %collective-permute-start) | collective-permute-done | bytes 262176 | tf_op jit(solution)/shard_map/ppermute | solution.py:23
  4.5 0.0 copy-start
  4.5 1.2 %copy-done = bf16[256,2048]{1,0:T(8,128)(2,1)S(1)} copy-done((bf16[256,2048]{1,0:T(8,128)(2,1)S(1)}, bf16[256,2048]{1,0:T(8,128)(2,1)}, u32[]{:S(2)}) %copy-start) | copy-done | bytes 1048600
  5.7 0.0 copy-start.1
  5.7 0.8 %copy-done.1 = s32[256,64]{0,1:T(8,128)S(1)} copy-done((s32[256,64]{0,1:T(8,128)S(1)}, s32[256,64]{0,1:T(8,128)}, u32[]{:S(2)}) %copy-start.1) | copy-done | bytes 65560
  6.6 8.2 %dedisperse.1 = (f32[64,2432]{1,0:T(8,128)S(1)}, s16[64,2432]{1,0:T(8,128)(2,1)S(1)}) custom-call(bf16[256,512]{1,0:T(8,128)(2,1)S(1)} %collective-permute-done.rim_ref, bf16[256,2048]{1,0:T(8,128)(2,1)S(1)} %copy-done, s32[64,256]{1,0:T(8,128)S(1)} %bitcast.8), custom_call_target="tpu_custom_call" | custom-call | tf_op jit(solution)/shard_map/dedisperse/pallas_call | solution.py:101
  14.8 2.4 %collective-permute-start.1 = (s16[64,2432]{1,0:T(8,128)(2,1)S(1)}, s16[64,2432]{1,0:T(8,128)(2,1)S(1)}, u32[]{:S(2)}, u32[]{:S(2)}) collective-permute-start(s16[64,2432]{1,0:T(8,128)(2,1)S(1)} %get-tuple-element.14), channel_id=1, source_target_pairs={{0,2},{2,0},{4,6},{6,4},{8,10},{10,8},{12,14},{14,12},{1,3},{3,1},... | collective-permute-start | bytes 933896 | tf_op jit(solution)/shard_map/ppermute | solution.py:27
  17.2 0.7 %pad_add_fusion = s32[9,64]{1,0:T(8,128)S(1)} fusion(s32[3,64]{1,0:T(4,128)} %param.10, s32[3,64]{1,0:T(4,128)} %param.9, s32[3,64]{1,0:T(4,128)} %param.8), kind=kLoop, calls=%fused_computation | loop fusion | flops 1152 | bytes 4608 | tf_op jit(solution)/shard_map/concatenate | solution.py:238
  18.0 0.1 copy.10
  18.1 7.1 %collective-permute-done.1.coded_ref = s16[64,2432]{1,0:T(8,128)(2,1)S(1)} collective-permute-done((s16[64,2432]{1,0:T(8,128)(2,1)S(1)}, s16[64,2432]{1,0:T(8,128)(2,1)S(1)}, u32[]{:S(2)}, u32[]{:S(2)}) %collective-permute-start.1) | collective-permute-done | bytes 311328 | tf_op jit(solution)/shard_map/ppermute | solution.py:27
  25.1 1.6 %merge_0.1 = (f32[64,2432]{1,0:T(8,128)S(1)}, s16[64,2432]{1,0:T(8,128)(2,1)S(1)}) custom-call(s32[1]{0:T(128)} %bitcast.2.side_ref, f32[64,2432]{1,0:T(8,128)S(1)} %get-tuple-element.13.own_ref, s16[64,2432]{1,0:T(8,128)(2,1)S(1)} %collective-permute-done.1.coded_ref, s32[64,9]{1,0:T(8,128)S(1)} %bitcast.5), custom_call_target="tpu_custom_call" | custom-call | tf_op jit(solution)/shard_map/merge_0/pallas_call | solution.py:163
  26.7 1.9 %collective-permute-start.2 = (s16[64,2432]{1,0:T(8,128)(2,1)S(1)}, s16[64,2432]{1,0:T(8,128)(2,1)S(1)}, u32[]{:S(2)}, u32[]{:S(2)}) collective-permute-start(s16[64,2432]{1,0:T(8,128)(2,1)S(1)} %get-tuple-element.16), channel_id=1, source_target_pairs={{0,4},{2,6},{4,0},{6,2},{8,12},{10,14},{12,8},{14,10},{1,5},{3,7},... | collective-permute-start | bytes 933896 | tf_op jit(solution)/shard_map/ppermute | solution.py:27
  28.6 7.3 %collective-permute-done.2.coded_ref = s16[64,2432]{1,0:T(8,128)(2,1)S(1)} collective-permute-done((s16[64,2432]{1,0:T(8,128)(2,1)S(1)}, s16[64,2432]{1,0:T(8,128)(2,1)S(1)}, u32[]{:S(2)}, u32[]{:S(2)}) %collective-permute-start.2) | collective-permute-done | bytes 311328 | tf_op jit(solution)/shard_map/ppermute | solution.py:27
  35.8 1.8 %merge_1.1 = (f32[64,2304]{1,0:T(8,128)S(1)}, s16[64,2304]{1,0:T(8,128)(2,1)S(1)}) custom-call(s32[1]{0:T(128)} %bitcast.1.side_ref, f32[64,2432]{1,0:T(8,128)S(1)} %get-tuple-element.15.own_ref, s16[64,2432]{1,0:T(8,128)(2,1)S(1)} %collective-permute-done.2.coded_ref, s32[64,9]{1,0:T(8,128)S(1)} %bitcast.6), custom_call_target="tpu_custom_call" | custom-call | tf_op jit(solution)/shard_map/merge_1/pallas_call | solution.py:163
  37.6 2.6 %collective-permute-start.3 = (s16[64,2304]{1,0:T(8,128)(2,1)S(1)}, s16[64,2304]{1,0:T(8,128)(2,1)S(1)}, u32[]{:S(2)}, u32[]{:S(2)}) collective-permute-start(s16[64,2304]{1,0:T(8,128)(2,1)S(1)} %get-tuple-element.18), channel_id=1, source_target_pairs={{0,8},{2,10},{4,12},{6,14},{8,0},{10,2},{12,4},{14,6},{1,9},{3,11}... | collective-permute-start | bytes 884744 | tf_op jit(solution)/shard_map/ppermute | solution.py:27
  40.2 12.5 %collective-permute-done.3.coded_ref = s16[64,2304]{1,0:T(8,128)(2,1)S(1)} collective-permute-done((s16[64,2304]{1,0:T(8,128)(2,1)S(1)}, s16[64,2304]{1,0:T(8,128)(2,1)S(1)}, u32[]{:S(2)}, u32[]{:S(2)}) %collective-permute-start.3) | collective-permute-done | bytes 294944 | tf_op jit(solution)/shard_map/ppermute | solution.py:27
  52.7 1.9 %merge_2.1 = (f32[64,2176]{1,0:T(8,128)S(1)}, f32[64,1]{1,0:T(8,128)S(1)}) custom-call(s32[1]{0:T(128)} %bitcast.side_ref, f32[64,2304]{1,0:T(8,128)S(1)} %get-tuple-element.17.own_ref, s16[64,2304]{1,0:T(8,128)(2,1)S(1)} %collective-permute-done.3.coded_ref, s32[64,9]{1,0:T(8,128)S(1)} %bitcast.7), custom_call_target="tpu_custom_call" | custom-call | tf_op jit(solution)/shard_map/merge_2/pallas_call | solution.py:163
  54.6 3.4 %psum.7.squares_ref = f32[64,1]{1,0:T(8,128)S(1)} all-reduce(f32[64,1]{1,0:T(8,128)S(1)} %get-tuple-element.20), channel_id=1, replica_groups=mesh['beam'=2,'chan'=8,'tm'=2] {'tm'}, use_global_device_ids=true, to_apply=%region_0.0 | all-reduce | flops 64 | bytes 512 | tf_op jit(solution)/shard_map/psum | solution.py:244
  58.0 0.0 copy-done.2
  58.0 3.9 %boxes.1 = f32[8,64,2048]{2,1,0:T(8,128)} custom-call(s32[8]{0:T(128)S(1)} %copy-done.2, f32[64,2176]{1,0:T(8,128)S(1)} %get-tuple-element.19.state_ref, f32[64,1]{1,0:T(8,128)S(1)} %psum.7.squares_ref), custom_call_target="tpu_custom_call" | custom-call | tf_op jit(solution)/shard_map/boxes/pallas_call | solution.py:214
Async XLA Ops:
  0.0 58.0 %copy-start.2 = (s32[8]{0:T(128)S(1)}, s32[8]{0:T(128)}, u32[]{:S(2)}) copy-start(s32[8]{0:T(128)} %widths_ref.1) | copy-start | bytes 100
  1.0 3.5 %collective-permute-start = (bf16[256,512]{1,0:T(8,128)(2,1)S(1)}, bf16[256,512]{1,0:T(8,128)(2,1)S(1)}, u32[]{:S(2)}, u32[]{:S(2)}) collective-permute-start(bf16[256,512]{1,0:T(8,128)(2,1)S(1)} %slice.3), channel_id=1, source_target_pairs={{0,1},{2,3},{4,5},{6,7},{8,9},{10,11},{12,13},{14,15},{16,17},{18,... | collective-permute-start | bytes 786440 | tf_op jit(solution)/shard_map/ppermute | solution.py:23
  4.5 1.2 %copy-start = (bf16[256,2048]{1,0:T(8,128)(2,1)S(1)}, bf16[256,2048]{1,0:T(8,128)(2,1)}, u32[]{:S(2)}) copy-start(bf16[256,2048]{1,0:T(8,128)(2,1)} %fb_ref.1) | copy-start | bytes 3145732
  5.7 0.8 %copy-start.1 = (s32[256,64]{0,1:T(8,128)S(1)}, s32[256,64]{0,1:T(8,128)}, u32[]{:S(2)}) copy-start(s32[256,64]{0,1:T(8,128)} %param.7) | copy-start | bytes 196612
  14.8 10.3 %collective-permute-start.1 = (s16[64,2432]{1,0:T(8,128)(2,1)S(1)}, s16[64,2432]{1,0:T(8,128)(2,1)S(1)}, u32[]{:S(2)}, u32[]{:S(2)}) collective-permute-start(s16[64,2432]{1,0:T(8,128)(2,1)S(1)} %get-tuple-element.14), channel_id=1, source_target_pairs={{0,2},{2,0},{4,6},{6,4},{8,10},{10,8},{12,14},{14,12},{1,3},{3,1},... | collective-permute-start | bytes 933896 | tf_op jit(solution)/shard_map/ppermute | solution.py:27
  26.7 9.1 %collective-permute-start.2 = (s16[64,2432]{1,0:T(8,128)(2,1)S(1)}, s16[64,2432]{1,0:T(8,128)(2,1)S(1)}, u32[]{:S(2)}, u32[]{:S(2)}) collective-permute-start(s16[64,2432]{1,0:T(8,128)(2,1)S(1)} %get-tuple-element.16), channel_id=1, source_target_pairs={{0,4},{2,6},{4,0},{6,2},{8,12},{10,14},{12,8},{14,10},{1,5},{3,7},... | collective-permute-start | bytes 933896 | tf_op jit(solution)/shard_map/ppermute | solution.py:27
  37.6 15.1 %collective-permute-start.3 = (s16[64,2304]{1,0:T(8,128)(2,1)S(1)}, s16[64,2304]{1,0:T(8,128)(2,1)S(1)}, u32[]{:S(2)}, u32[]{:S(2)}) collective-permute-start(s16[64,2304]{1,0:T(8,128)(2,1)S(1)} %get-tuple-element.18), channel_id=1, source_target_pairs={{0,8},{2,10},{4,12},{6,14},{8,0},{10,2},{12,4},{14,6},{1,9},{3,11}... | collective-permute-start | bytes 884744 | tf_op jit(solution)/shard_map/ppermute | solution.py:27

commit v2 on v1

v2 whole, which is shorter than its diff:
```python
import functools

import jax
import jax.numpy as jnp
from jax import lax
from jax.experimental import pallas as pl
from jax.experimental.pallas import tpu as pltpu
from jax.sharding import PartitionSpec as P

DLOC = 64
LANES = 128
FINE = 8
COARSE = DLOC // FINE
CHUNKS = 3
MESH = pl.DeviceIdType.MESH


def lane_up(count):
    return -(-count // LANES) * LANES


def code_rows(rows, lead):
    largest = jnp.maximum(jnp.max(jnp.abs(rows), axis=1, keepdims=True), 2.0**-100)
    exponent = jnp.floor(jnp.log2(largest))
    coded = jnp.round(jnp.clip(rows * jnp.exp2(14.0 - exponent), -32767.0, 32767.0))
    if lead:
        front = jnp.broadcast_to(exponent, (rows.shape[0], lead))
        coded = jnp.concatenate([front, coded], axis=1)
    else:
        column = lax.broadcasted_iota(jnp.int32, rows.shape, 1)
        coded = jnp.where(column == 0, exponent, coded)
    return coded.astype(jnp.int32).astype(jnp.int16)


def decode_rows(coded, lead):
    values = coded.astype(jnp.int32).astype(jnp.float32)
    return values[:, lead:] * jnp.exp2(values[:, :1] - 14.0)


def as_column(row):
    count = row.shape[1]
    at = lax.broadcasted_iota(jnp.int32, (count, count), 0)
    to = lax.broadcasted_iota(jnp.int32, (count, count), 1)
    spread = jnp.where(at == to, row.astype(jnp.float32), 0.0)
    return jnp.sum(spread, axis=1, keepdims=True).astype(jnp.int32)


def pick(index, source):
    rows = source.shape[0]
    at = lax.broadcasted_iota(jnp.int32, (index.shape[0], rows), 1)
    once = jnp.where(at == index, 1.0, 0.0).astype(jnp.bfloat16)
    chosen = jnp.concatenate([once, once], axis=1)
    high = source.astype(jnp.bfloat16)
    low = (source - high.astype(jnp.float32)).astype(jnp.bfloat16)
    return jnp.dot(
        chosen, jnp.concatenate([high, low], axis=0), preferred_element_type=jnp.float32
    )


def sweep_kernel(
    edges,
    starts,
    rim,
    fb_ref,
    delays_ref,
    lower_ref,
    upper_ref,
    shifts_ref,
    state_ref,
    squares_ref,
    ext,
    onehot,
    spread,
    partial,
    owns,
    picked,
    outgoing,
    incoming,
    square_out,
    square_in,
    local_sem,
    pair_send,
    pair_recv,
    send_sem,
    recv_sem,
):
    channels, samples = fb_ref.shape
    rows = delays_ref.shape[0]
    levels = len(owns)
    chunks = len(edges) - 1
    width = edges[-1]
    total = rim + samples
    skip = total - width
    tail = picked[0].shape[1] - width
    sent_rim = min(rim, samples)
    empty = LANES + rim - sent_rim

    chan = lax.axis_index("chan")
    tm = lax.axis_index("tm")
    sides = [lax.rem(lax.div(chan, 1 << level), 2) for level in range(levels)]
    partners = [
        {"chan": chan + (1 << level) - (2 << level) * sides[level]} for level in range(levels)
    ]
    pair = {"tm": 1 - tm}

    barrier = pltpu.get_barrier_semaphore()
    for device in [pair] + partners:
        pl.semaphore_signal(barrier, inc=1, device_id=device, device_id_type=MESH)
    own_copy = pltpu.make_async_copy(fb_ref, ext.at[:, pl.ds(LANES + rim, samples)], local_sem)
    own_copy.start()
    pl.semaphore_wait(barrier, levels + 1)
    rim_copy = pltpu.make_async_remote_copy(
        src_ref=fb_ref.at[:, pl.ds(samples - sent_rim, sent_rim)],
        dst_ref=ext.at[:, pl.ds(empty, sent_rim)],
        send_sem=pair_send.at[0],
        recv_sem=pair_recv.at[0],
        device_id=pair,
        device_id_type=MESH,
    )
    rim_copy.start()

    ext[:, :empty] = jnp.zeros((channels, empty), jnp.bfloat16)
    for level in range(levels):
        picked[level][:, :tail] = jnp.zeros((rows, tail), jnp.float32)
    for coarse in range(COARSE):
        relative = delays_ref[...] - FINE * coarse
        for fine in range(FINE):
            onehot[coarse * rows : (coarse + 1) * rows, fine * channels : (fine + 1) * channels] = (
                jnp.where(relative == fine, 1.0, 0.0).astype(jnp.bfloat16)
            )
    lows = [as_column(lower_ref[level : level + 1, :]) for level in range(levels)]
    highs = [as_column(upper_ref[level : level + 1, :]) for level in range(levels)]
    shifts = [as_column(shifts_ref[level : level + 1, :]) for level in range(levels)]

    def exchange(level, chunk):
        return pltpu.make_async_remote_copy(
            src_ref=outgoing[level][chunk],
            dst_ref=incoming[level][chunk],
            send_sem=send_sem.at[level, chunk],
            recv_sem=recv_sem.at[level, chunk],
            device_id=partners[level],
            device_id_type=MESH,
        )

    def lead(chunk):
        return LANES if chunk else 0

    def first_of(level, chunk):
        return max(edges[chunk], starts[level])

    def hand_on(level, chunk, values):
        owns[level][:, first_of(level, chunk) : edges[chunk + 1]] = values
        outgoing[level][chunk][...] = code_rows(values, lead(chunk))
        exchange(level, chunk).start()

    def dedisperse(chunk):
        begin = skip + edges[chunk] if chunk else 0
        end = skip + edges[chunk + 1]
        tile = 2 * LANES if (end - begin) % (2 * LANES) == 0 else LANES

        def step(index, carry):
            start = pl.multiple_of(begin + index * tile, LANES)
            window = ext[:, pl.ds(start, tile + LANES)]
            for fine in range(FINE):
                spread[fine * channels : (fine + 1) * channels, :tile] = window[
                    :, LANES - fine : LANES - fine + tile
                ]
            partial[:, pl.ds(start, tile)] = jnp.dot(
                onehot[...], spread[:, :tile], preferred_element_type=jnp.float32
            )
            return carry

        lax.fori_loop(0, (end - begin) // tile, step, 0)
        summed = None
        for coarse in range(COARSE):
            back = skip - FINE * coarse
            term = partial[
                coarse * rows : (coarse + 1) * rows, back + edges[chunk] : back + edges[chunk + 1]
            ]
            summed = term if summed is None else summed + term
        hand_on(0, chunk, summed)

    def merge(level, chunk):
        begin, end = first_of(level, chunk), edges[chunk + 1]
        exchange(level, chunk).wait_recv()
        own = owns[level][:, begin:end]
        partner = decode_rows(incoming[level][chunk][...], lead(chunk))
        upper_side = sides[level] == 1
        low = pick(lows[level], jnp.where(upper_side, partner, own))
        high = pick(highs[level], jnp.where(upper_side, own, partner))
        reach = DLOC * 2**level // 2
        room = lane_up(reach)
        picked[level][:, tail + begin : tail + end] = high
        moved = picked[level][:, tail + begin - room : tail + end]
        for bit in range((reach - 1).bit_length()):
            moved = jnp.where(
                (shifts[level] >> bit) & 1 == 1, pltpu.roll(moved, 2**bit, 1), moved
            )
        after = max(edges[chunk], starts[level + 1])
        return (low + moved[:, room:])[:, after - begin :]

    own_copy.wait()
    rim_copy.wait()
    ext[:, empty : LANES + rim] = jnp.where(
        tm == 0, jnp.zeros((channels, sent_rim), jnp.bfloat16), ext[:, empty : LANES + rim]
    )
    squares = jnp.zeros((rows, 1), jnp.float32)
    for turn in range(chunks + levels):
        if turn < chunks:
            dedisperse(turn)
        for level in range(levels):
            chunk = turn - 1 - level
            if not 0 <= chunk < chunks:
                continue
            merged = merge(level, chunk)
            if level < levels - 1:
                hand_on(level + 1, chunk, merged)
            else:
                begin = first_of(levels, chunk)
                state_ref[:, begin - starts[levels] : edges[chunk + 1] - starts[levels]] = merged
                if edges[chunk + 1] > width - samples:
                    fresh = merged[:, max(width - samples - begin, 0) :]
                    squares = squares + jnp.sum(fresh * fresh, axis=1, keepdims=True)
    square_out[...] = jnp.broadcast_to(squares, (rows, LANES))
    square_copy = pltpu.make_async_remote_copy(
        src_ref=square_out,
        dst_ref=square_in,
        send_sem=pair_send.at[1],
        recv_sem=pair_recv.at[1],
        device_id=pair,
        device_id_type=MESH,
    )
    square_copy.start()
    for level in range(levels):
        for chunk in range(chunks):
            exchange(level, chunk).wait_send()
    square_copy.wait()
    squares_ref[...] = square_out[...] + square_in[...]


def sweep(filterbank, delays, lower_rows, upper_rows, level_shifts, widths):
    channels, samples = filterbank.shape
    rows = delays.shape[0]
    levels = len(widths) - 1
    width = widths[0]
    rim = lane_up(width - samples + DLOC - 1)
    total = rim + samples
    starts = [width - each for each in widths]
    tiles = width // LANES
    fair = (tiles - 1) // CHUNKS
    most = (widths[-1] // LANES - 1) // max(CHUNKS - 1, 1)
    later = min(fair, most) // 2 * 2 or 1
    sizes = [tiles - later * (CHUNKS - 1)] + [later] * (CHUNKS - 1)
    edges = [LANES * sum(sizes[:count]) for count in range(CHUNKS + 1)]

    def coded():
        return [
            [
                pltpu.VMEM(
                    (rows, edges[c + 1] - max(edges[c], starts[j]) + (LANES if c else 0)),
                    jnp.int16,
                )
                for c in range(CHUNKS)
            ]
            for j in range(levels)
        ]

    tail = lane_up(DLOC * 2 ** (levels - 1) // 2)
    vmem = pl.BlockSpec(memory_space=pltpu.VMEM)
    return pl.pallas_call(
        functools.partial(sweep_kernel, edges, starts, rim),
        name="sweep",
        out_shape=(
            jax.ShapeDtypeStruct((rows, widths[-1]), jnp.float32),
            jax.ShapeDtypeStruct((rows, LANES), jnp.float32),
        ),
        in_specs=[pl.BlockSpec(memory_space=pltpu.HBM), vmem, vmem, vmem, vmem],
        out_specs=(vmem, vmem),
        scratch_shapes=[
            pltpu.VMEM((channels, LANES + total), jnp.bfloat16),
            pltpu.VMEM((COARSE * rows, FINE * channels), jnp.bfloat16),
            pltpu.VMEM((FINE * channels, 2 * LANES), jnp.bfloat16),
            pltpu.VMEM((COARSE * rows, total), jnp.float32),
            [pltpu.VMEM((rows, width), jnp.float32) for _ in range(levels)],
            [pltpu.VMEM((rows, tail + width), jnp.float32) for _ in range(levels)],
            coded(),
            coded(),
            pltpu.VMEM((rows, LANES), jnp.float32),
            pltpu.VMEM((rows, LANES), jnp.float32),
            pltpu.SemaphoreType.DMA,
            pltpu.SemaphoreType.DMA((2,)),
            pltpu.SemaphoreType.DMA((2,)),
            pltpu.SemaphoreType.DMA((levels, CHUNKS)),
            pltpu.SemaphoreType.DMA((levels, CHUNKS)),
        ],
        compiler_params=pltpu.CompilerParams(
            collective_id=0, has_side_effects=True, vmem_limit_bytes=48 * 2**20
        ),
    )(filterbank, delays, lower_rows, upper_rows, level_shifts)


def box_kernel(times, widths_ref, state_ref, squares_ref, out_ref, stacked):
    rows = state_ref.shape[0]
    tiles = out_ref.shape[2] // LANES
    per_step = out_ref.shape[0]

    @pl.when(pl.program_id(0) == 0)
    def _():
        for tile in range(tiles):
            part = state_ref[:, tile * LANES : (tile + 2) * LANES]
            high = part.astype(jnp.bfloat16)
            low = (part - high.astype(jnp.float32)).astype(jnp.bfloat16)
            stacked[tile * rows : (tile + 1) * rows, : 2 * LANES] = high
            stacked[tile * rows : (tile + 1) * rows, 2 * LANES :] = low

    inverse = lax.rsqrt(squares_ref[...] / times + 1e-05)
    masks = []
    factors = []
    for which in range(per_step):
        box_width = widths_ref[pl.program_id(0) * per_step + which]
        at = lax.broadcasted_iota(jnp.int32, (2 * LANES, LANES), 0) - LANES
        to = lax.broadcasted_iota(jnp.int32, (2 * LANES, LANES), 1)
        inside = (at <= to) & (at > to - box_width)
        mask = jnp.where(inside, 1.0, 0.0).astype(jnp.bfloat16)
        masks.append(jnp.concatenate([mask, mask], axis=0))
        root = jnp.sqrt(jnp.full((rows, LANES), box_width.astype(jnp.float32)))
        factors.append(inverse / root)
    boxes = jnp.dot(
        stacked[...], jnp.concatenate(masks, axis=1), preferred_element_type=jnp.float32
    )
    for which in range(per_step):
        for tile in range(tiles):
            out_ref[which, :, tile * LANES : (tile + 1) * LANES] = (
                boxes[tile * rows : (tile + 1) * rows, which * LANES : (which + 1) * LANES]
                * factors[which]
            )


def box_filter(widths, state, squares, samples, times):
    rows = state.shape[0]
    count = widths.shape[0]
    per_step = 2 if count % 2 == 0 else 1
    return pl.pallas_call(
        functools.partial(box_kernel, times),
        name="boxes",
        grid=(count // per_step,),
        out_shape=jax.ShapeDtypeStruct((count, rows, samples), jnp.float32),
        in_specs=[
            pl.BlockSpec(memory_space=pltpu.SMEM),
            pl.BlockSpec(memory_space=pltpu.VMEM),
            pl.BlockSpec(memory_space=pltpu.VMEM),
        ],
        out_specs=pl.BlockSpec((per_step, rows, samples), lambda i: (i, 0, 0)),
        scratch_shapes=[pltpu.VMEM((samples // LANES * rows, 4 * LANES), jnp.bfloat16)],
        compiler_params=pltpu.CompilerParams(vmem_limit_bytes=32 * 2**20),
    )(widths, state, squares)


def local(filterbank, local_delays, lower_rows, upper_rows, level_shifts, box_widths):
    samples = filterbank.shape[1]
    levels = lax.axis_size("chan").bit_length() - 1
    needs = [LANES]
    for level in reversed(range(levels)):
        needs.insert(0, needs[0] - (level == levels - 1) + DLOC * 2**level // 2 - 1)
    widths = [samples + lane_up(need + 1) for need in needs[:-1]] + [samples + LANES]
    state, squares = sweep(
        filterbank, local_delays.T, lower_rows, upper_rows, level_shifts, widths
    )
    return box_filter(box_widths, state, squares, samples, samples * lax.axis_size("tm"))


def solution(mesh):
    placed = (
        P(("beam", "chan"), "tm"),
        P("chan", None),
        P(None, "chan"),
        P(None, "chan"),
        P(None, "chan"),
        P(),
    )
    return jax.shard_map(
        local,
        mesh=mesh,
        in_specs=placed,
        out_specs=P(None, ("beam", "chan"), "tm"),
        check_vma=False,
    )
```

time: 62.2 us -> 47.1 us (0.76)
  waiting for transfers between devices: 27.9 us -> 0 us
  Pallas kernels: 17.4 us -> 42 us
  starting transfers between devices: 9.3 us -> 0 us
  blocking collectives: 3.4 us -> 0 us
  local copies, waits for them, and re-layouts: 3.14 us -> 4.76 us
  other arithmetic: 0.72 us -> 0 us
    ppermute x4 -> x0, waiting for transfers between devices: 27.9 us -> none  [the longest x3 26.8 us: from_partner(): lax.ppermute(array, axis, [(i, i ^ 1 << distance) for i in range(lax.axis...]
    pallas_call x4 -> x1, Pallas kernels: 13.5 us -> 38.1 us  [sweep(): pl.pallas_call(functools.partial(sweep_kernel, edges, starts, rim), name=...]
    ppermute x4 -> x0, starting transfers between devices: 9.3 us -> none  [the longest x3 6.93 us: from_partner(): lax.ppermute(array, axis, [(i, i ^ 1 << distance) for i in range(lax.axis...]
    psum x1 -> x0, blocking collectives: 3.4 us -> none  [local(): squares = lax.psum(coded, 'tm')]
    unnamed x6 -> x12, local copies, waits for them, and re-layouts: 2.07 us -> 4.76 us
    slice x1 -> x0, local copies, waits for them, and re-layouts: 0.98 us -> none  [left_context(): pieces.insert(0, from_earlier(block[:, samples - part:], axis, distance))]
    concatenate x1 -> x0, other arithmetic: 0.72 us -> none  [local(): plan = jnp.concatenate([lower_rows, upper_rows, level_shifts], axis=0).T]
  transfers between devices with their start and end apart: 4 -> 0, of which waited for: 4 -> 0; matrix products, arithmetic and copies ran while one was open for 1% -> 0% of each run, Pallas kernels for 0% -> 0%
where the time goes in v2:
time: 47.1 us; the launch traced here: 46.8 us
  Pallas kernels  42 us (89%)
  local copies, waits for them, and re-layouts  4.76 us (10%)
    pallas_call x1, Pallas kernels, sweep(): pl.pallas_call(functools.partial(sweep_kernel, edges, starts, rim), name=...  38.1 us
    unnamed x12, local copies, waits for them, and re-layouts  4.76 us
    pallas_call x1, Pallas kernels, box_filter(): pl.pallas_call(functools.partial(box_kernel, times), name='boxes', grid=(...  3.93 us

profile of v2, /device:TPU:0, one launch (start us, length us, event | category | flops | bytes accessed | tf_op | source)
XLA Modules:
  0.0 46.8 jit_solution(9801803270827315758)
XLA Ops:
  0.0 0.0 copy-start
  0.0 1.2 %copy-done = bf16[256,2048]{1,0:T(8,128)(2,1)S(1)} copy-done((bf16[256,2048]{1,0:T(8,128)(2,1)S(1)}, bf16[256,2048]{1,0:T(8,128)(2,1)}, u32[]{:S(2)}) %copy-start) | copy-done | bytes 1048600
  1.2 0.0 copy-start.1
  1.2 0.8 %copy-done.1 = s32[256,64]{0,1:T(8,128)S(1)} copy-done((s32[256,64]{0,1:T(8,128)S(1)}, s32[256,64]{0,1:T(8,128)}, u32[]{:S(2)}) %copy-start.1) | copy-done | bytes 65560
  2.1 0.0 copy-start.2
  2.1 0.7 %copy-done.2 = s32[3,64]{1,0:T(4,128)S(1)} copy-done((s32[3,64]{1,0:T(4,128)S(1)}, s32[3,64]{1,0:T(4,128)}, u32[]{:S(2)}) %copy-start.2) | copy-done | bytes 792
  2.7 0.0 copy-start.3
  2.8 0.7 %copy-done.3 = s32[3,64]{1,0:T(4,128)S(1)} copy-done((s32[3,64]{1,0:T(4,128)S(1)}, s32[3,64]{1,0:T(4,128)}, u32[]{:S(2)}) %copy-start.3) | copy-done | bytes 792
  3.4 0.0 copy-start.4
  3.4 0.7 %copy-done.4 = s32[3,64]{1,0:T(4,128)S(1)} copy-done((s32[3,64]{1,0:T(4,128)S(1)}, s32[3,64]{1,0:T(4,128)}, u32[]{:S(2)}) %copy-start.4) | copy-done | bytes 792
  4.1 38.1 %sweep.1 = (f32[64,2176]{1,0:T(8,128)S(1)}, f32[64,128]{1,0:T(8,128)S(1)}) custom-call(bf16[256,2048]{1,0:T(8,128)(2,1)S(1)} %copy-done, s32[64,256]{1,0:T(8,128)S(1)} %bitcast.1, s32[3,64]{1,0:T(4,128)S(1)} %copy-done.2, s32[3,64]{1,0:T(4,128)S(1)} %copy-done.3, s32[3,64]{1,0:T(4,128)S(1)} %copy-done.4), custom_call_target="tpu_custom_call" | custom-call | tf_op jit(solution)/shard_map/sweep/pallas_call | solution.py:270
  42.2 0.0 copy-start.5
  42.2 0.6 %copy-done.5 = s32[8]{0:T(128)S(1)} copy-done((s32[8]{0:T(128)S(1)}, s32[8]{0:T(128)}, u32[]{:S(2)}) %copy-start.5) | copy-done | bytes 56
  42.8 3.9 %boxes.1 = f32[8,64,2048]{2,1,0:T(8,128)} custom-call(s32[8]{0:T(128)S(1)} %copy-done.5, f32[64,2176]{1,0:T(8,128)S(1)} %get-tuple-element.7.state_ref, f32[64,128]{1,0:T(8,128)S(1)} %get-tuple-element.8.squares_ref), custom_call_target="tpu_custom_call" | custom-call | tf_op jit(solution)/shard_map/boxes/pallas_call | solution.py:343
Async XLA Ops:
  0.0 1.2 %copy-start = (bf16[256,2048]{1,0:T(8,128)(2,1)S(1)}, bf16[256,2048]{1,0:T(8,128)(2,1)}, u32[]{:S(2)}) copy-start(bf16[256,2048]{1,0:T(8,128)(2,1)} %fb_ref.1) | copy-start | bytes 3145732
  1.2 0.8 %copy-start.1 = (s32[256,64]{0,1:T(8,128)S(1)}, s32[256,64]{0,1:T(8,128)}, u32[]{:S(2)}) copy-start(s32[256,64]{0,1:T(8,128)} %param.7) | copy-start | bytes 196612
  2.1 0.7 %copy-start.2 = (s32[3,64]{1,0:T(4,128)S(1)}, s32[3,64]{1,0:T(4,128)}, u32[]{:S(2)}) copy-start(s32[3,64]{1,0:T(4,128)} %lower_ref.1) | copy-start | bytes 2308
  2.7 0.7 %copy-start.3 = (s32[3,64]{1,0:T(4,128)S(1)}, s32[3,64]{1,0:T(4,128)}, u32[]{:S(2)}) copy-start(s32[3,64]{1,0:T(4,128)} %upper_ref.1) | copy-start | bytes 2308
  3.4 0.7 %copy-start.4 = (s32[3,64]{1,0:T(4,128)S(1)}, s32[3,64]{1,0:T(4,128)}, u32[]{:S(2)}) copy-start(s32[3,64]{1,0:T(4,128)} %shifts_ref.1) | copy-start | bytes 2308
  42.2 0.7 %copy-start.5 = (s32[8]{0:T(128)S(1)}, s32[8]{0:T(128)}, u32[]{:S(2)}) copy-start(s32[8]{0:T(128)} %widths_ref.1) | copy-start | bytes 100

commit v3 on v2

--- a/solution.py
+++ b/solution.py
@@ -12,6 +12,7 @@
 FINE = 8
 COARSE = DLOC // FINE
 CHUNKS = 3
+PACKED = 16
 MESH = pl.DeviceIdType.MESH
 
 
@@ -19,22 +20,21 @@
     return -(-count // LANES) * LANES
 
 
-def code_rows(rows, lead):
+def code_rows(rows):
     largest = jnp.maximum(jnp.max(jnp.abs(rows), axis=1, keepdims=True), 2.0**-100)
     exponent = jnp.floor(jnp.log2(largest))
     coded = jnp.round(jnp.clip(rows * jnp.exp2(14.0 - exponent), -32767.0, 32767.0))
-    if lead:
-        front = jnp.broadcast_to(exponent, (rows.shape[0], lead))
-        coded = jnp.concatenate([front, coded], axis=1)
-    else:
-        column = lax.broadcasted_iota(jnp.int32, rows.shape, 1)
-        coded = jnp.where(column == 0, exponent, coded)
-    return coded.astype(jnp.int32).astype(jnp.int16)
-
-
-def decode_rows(coded, lead):
+    at = lax.broadcasted_iota(jnp.int32, (rows.shape[0], LANES), 0)
+    to = lax.broadcasted_iota(jnp.int32, (rows.shape[0], LANES), 1)
+    along = jnp.sum(jnp.where(at == to, exponent, 0.0), axis=0, keepdims=True)
+    along = jnp.broadcast_to(along, (PACKED, LANES))
+    return coded.astype(jnp.int32).astype(jnp.int16), along.astype(jnp.int32).astype(jnp.int16)
+
+
+def decode_rows(coded, along):
     values = coded.astype(jnp.int32).astype(jnp.float32)
-    return values[:, lead:] * jnp.exp2(values[:, :1] - 14.0)
+    exponents = along.astype(jnp.int32)[:1, : coded.shape[0]]
+    return values * jnp.exp2(as_column(exponents).astype(jnp.float32) - 14.0)
 
 
 def as_column(row):
@@ -62,12 +62,19 @@
     starts,
     rim,
     fb_ref,
+    delays_hbm,
+    lower_hbm,
+    upper_hbm,
+    shifts_hbm,
+    widths_hbm,
+    state_ref,
+    squares_ref,
+    widths_ref,
     delays_ref,
     lower_ref,
     upper_ref,
     shifts_ref,
-    state_ref,
-    squares_ref,
+    widths_row,
     ext,
     onehot,
     spread,
@@ -76,13 +83,18 @@
     picked,
     outgoing,
     incoming,
+    scale_out,
+    scale_in,
     square_out,
     square_in,
     local_sem,
+    small_sem,
     pair_send,
     pair_recv,
     send_sem,
     recv_sem,
+    scale_send,
+    scale_recv,
 ):
     channels, samples = fb_ref.shape
     rows = delays_ref.shape[0]
@@ -107,6 +119,20 @@
     for device in [pair] + partners:
         pl.semaphore_signal(barrier, inc=1, device_id=device, device_id_type=MESH)
     own_copy = pltpu.make_async_copy(fb_ref, ext.at[:, pl.ds(LANES + rim, samples)], local_sem)
+    small_copies = [
+        pltpu.make_async_copy(source, target, small_sem.at[at])
+        for at, (source, target) in enumerate(
+            [
+                (delays_hbm, delays_ref),
+                (lower_hbm, lower_ref),
+                (upper_hbm, upper_ref),
+                (shifts_hbm, shifts_ref),
+                (widths_hbm, widths_row),
+            ]
+        )
+    ]
+    for copy in small_copies:
+        copy.start()
     own_copy.start()
     pl.semaphore_wait(barrier, levels + 1)
     rim_copy = pltpu.make_async_remote_copy(
@@ -122,6 +148,9 @@
     ext[:, :empty] = jnp.zeros((channels, empty), jnp.bfloat16)
     for level in range(levels):
         picked[level][:, :tail] = jnp.zeros((rows, tail), jnp.float32)
+    for copy in small_copies:
+        copy.wait()
+    widths_ref[...] = jnp.broadcast_to(as_column(widths_row[...]), widths_ref.shape)
     for coarse in range(COARSE):
         relative = delays_ref[...] - FINE * coarse
         for fine in range(FINE):
@@ -132,26 +161,58 @@
     highs = [as_column(upper_ref[level : level + 1, :]) for level in range(levels)]
     shifts = [as_column(shifts_ref[level : level + 1, :]) for level in range(levels)]
 
-    def exchange(level, chunk):
-        return pltpu.make_async_remote_copy(
-            src_ref=outgoing[level][chunk],
-            dst_ref=incoming[level][chunk],
-            send_sem=send_sem.at[level, chunk],
-            recv_sem=recv_sem.at[level, chunk],
-            device_id=partners[level],
-            device_id_type=MESH,
-        )
-
-    def lead(chunk):
-        return LANES if chunk else 0
-
     def first_of(level, chunk):
         return max(edges[chunk], starts[level])
 
+    def history(level, chunk):
+        begin = first_of(level, chunk)
+        return min(max(width - samples - begin, 0), edges[chunk + 1] - begin)
+
+    def exchange(level, chunk, act):
+        old = history(level, chunk)
+        size = edges[chunk + 1] - first_of(level, chunk)
+
+        def columns(begin):
+            act(
+                pltpu.make_async_remote_copy(
+                    src_ref=outgoing[level][chunk].at[:, pl.ds(begin, size - begin)],
+                    dst_ref=incoming[level][chunk].at[:, pl.ds(begin, size - begin)],
+                    send_sem=send_sem.at[level, chunk],
+                    recv_sem=recv_sem.at[level, chunk],
+                    device_id=partners[level],
+                    device_id_type=MESH,
+                )
+            )
+
+        act(
+            pltpu.make_async_remote_copy(
+                src_ref=scale_out.at[level, chunk],
+                dst_ref=scale_in.at[level, chunk],
+                send_sem=scale_send.at[level, chunk],
+                recv_sem=scale_recv.at[level, chunk],
+                device_id=partners[level],
+                device_id_type=MESH,
+            )
+        )
+        if old:
+            pl.when(tm > 0)(lambda: columns(0))
+            if old < size:
+                pl.when(tm == 0)(lambda: columns(old))
+        else:
+            columns(0)
+
     def hand_on(level, chunk, values):
         owns[level][:, first_of(level, chunk) : edges[chunk + 1]] = values
-        outgoing[level][chunk][...] = code_rows(values, lead(chunk))
-        exchange(level, chunk).start()
+        outgoing[level][chunk][...], scale_out[level, chunk] = code_rows(values)
+        exchange(level, chunk, lambda copy: copy.start())
+
+    @pl.when(tm == 0)
+    def _():
+        for level in range(levels):
+            for chunk in range(chunks):
+                old = history(level, chunk)
+                if old:
+                    incoming[level][chunk][:, :old] = jnp.zeros((rows, old), jnp.int16)
 
     def dedisperse(chunk):
         begin = skip + edges[chunk] if chunk else 0
@@ -182,9 +243,9 @@
 
     def merge(level, chunk):
         begin, end = first_of(level, chunk), edges[chunk + 1]
-        exchange(level, chunk).wait_recv()
+        exchange(level, chunk, lambda copy: copy.wait_recv())
         own = owns[level][:, begin:end]
-        partner = decode_rows(incoming[level][chunk][...], lead(chunk))
+        partner = decode_rows(incoming[level][chunk][...], scale_in[level, chunk])
         upper_side = sides[level] == 1
         low = pick(lows[level], jnp.where(upper_side, partner, own))
         high = pick(highs[level], jnp.where(upper_side, own, partner))
@@ -233,12 +294,12 @@
     square_copy.start()
     for level in range(levels):
         for chunk in range(chunks):
-            exchange(level, chunk).wait_send()
+            exchange(level, chunk, lambda copy: copy.wait_send())
     square_copy.wait()
     squares_ref[...] = square_out[...] + square_in[...]
 
 
-def sweep(filterbank, delays, lower_rows, upper_rows, level_shifts, widths):
+def sweep(filterbank, delays, lower_rows, upper_rows, level_shifts, box_widths, widths):
     channels, samples = filterbank.shape
     rows = delays.shape[0]
     levels = len(widths) - 1
@@ -257,7 +318,7 @@
         return [
             [
                 pltpu.VMEM(
-                    (rows, edges[c + 1] - max(edges[c], starts[j]) + (LANES if c else 0)),
+                    (rows, edges[c + 1] - max(edges[c], starts[j])),
                     jnp.int16,
                 )
                 for c in range(CHUNKS)
@@ -273,10 +334,16 @@
         out_shape=(
             jax.ShapeDtypeStruct((rows, widths[-1]), jnp.float32),
             jax.ShapeDtypeStruct((rows, LANES), jnp.float32),
+            jax.ShapeDtypeStruct((box_widths.shape[0], LANES), jnp.int32),
         ),
-        in_specs=[pl.BlockSpec(memory_space=pltpu.HBM), vmem, vmem, vmem, vmem],
-        out_specs=(vmem, vmem),
+        in_specs=[pl.BlockSpec(memory_space=pltpu.HBM)] * 6,
+        out_specs=(vmem, vmem, vmem),
         scratch_shapes=[
+            pltpu.VMEM(delays.shape, jnp.int32),
+            pltpu.VMEM(lower_rows.shape, jnp.int32),
+            pltpu.VMEM(upper_rows.shape, jnp.int32),
+            pltpu.VMEM(level_shifts.shape, jnp.int32),
+            pltpu.VMEM((1, box_widths.shape[0]), jnp.int32),
             pltpu.VMEM((channels, LANES + total), jnp.bfloat16),
             pltpu.VMEM((COARSE * rows, FINE * channels), jnp.bfloat16),
             pltpu.VMEM((FINE * channels, 2 * LANES), jnp.bfloat16),
@@ -285,18 +352,23 @@
             [pltpu.VMEM((rows, tail + width), jnp.float32) for _ in range(levels)],
             coded(),
             coded(),
+            pltpu.VMEM((levels, CHUNKS, PACKED, LANES), jnp.int16),
+            pltpu.VMEM((levels, CHUNKS, PACKED, LANES), jnp.int16),
             pltpu.VMEM((rows, LANES), jnp.float32),
             pltpu.VMEM((rows, LANES), jnp.float32),
             pltpu.SemaphoreType.DMA,
+            pltpu.SemaphoreType.DMA((5,)),
             pltpu.SemaphoreType.DMA((2,)),
             pltpu.SemaphoreType.DMA((2,)),
+            pltpu.SemaphoreType.DMA((levels, CHUNKS)),
+            pltpu.SemaphoreType.DMA((levels, CHUNKS)),
             pltpu.SemaphoreType.DMA((levels, CHUNKS)),
             pltpu.SemaphoreType.DMA((levels, CHUNKS)),
         ],
         compiler_params=pltpu.CompilerParams(
             collective_id=0, has_side_effects=True, vmem_limit_bytes=48 * 2**20
         ),
-    )(filterbank, delays, lower_rows, upper_rows, level_shifts)
+    )(filterbank, delays, lower_rows, upper_rows, level_shifts, box_widths[None])
 
 
 def box_kernel(times, widths_ref, state_ref, squares_ref, out_ref, stacked):
@@ -317,13 +389,13 @@
     masks = []
     factors = []
     for which in range(per_step):
-        box_width = widths_ref[pl.program_id(0) * per_step + which]
+        box_width = widths_ref[pl.ds(pl.program_id(0) * per_step + which, 1), :]
         at = lax.broadcasted_iota(jnp.int32, (2 * LANES, LANES), 0) - LANES
         to = lax.broadcasted_iota(jnp.int32, (2 * LANES, LANES), 1)
         inside = (at <= to) & (at > to - box_width)
         mask = jnp.where(inside, 1.0, 0.0).astype(jnp.bfloat16)
         masks.append(jnp.concatenate([mask, mask], axis=0))
-        root = jnp.sqrt(jnp.full((rows, LANES), box_width.astype(jnp.float32)))
+        root = jnp.sqrt(box_width.astype(jnp.float32))
         factors.append(inverse / root)
     boxes = jnp.dot(
         stacked[...], jnp.concatenate(masks, axis=1), preferred_element_type=jnp.float32
@@ -346,7 +418,7 @@
         grid=(count // per_step,),
         out_shape=jax.ShapeDtypeStruct((count, rows, samples), jnp.float32),
         in_specs=[
-            pl.BlockSpec(memory_space=pltpu.SMEM),
+            pl.BlockSpec(memory_space=pltpu.VMEM),
             pl.BlockSpec(memory_space=pltpu.VMEM),
             pl.BlockSpec(memory_space=pltpu.VMEM),
         ],
@@ -363,10 +435,10 @@
     for level in reversed(range(levels)):
         needs.insert(0, needs[0] - (level == levels - 1) + DLOC * 2**level // 2 - 1)
     widths = [samples + lane_up(need + 1) for need in needs[:-1]] + [samples + LANES]
-    state, squares = sweep(
-        filterbank, local_delays.T, lower_rows, upper_rows, level_shifts, widths
-    )
-    return box_filter(box_widths, state, squares, samples, samples * lax.axis_size("tm"))
+    state, squares, spans = sweep(
+        filterbank, local_delays.T, lower_rows, upper_rows, level_shifts, box_widths, widths
+    )
+    return box_filter(spans, state, squares, samples, samples * lax.axis_size("tm"))
 
 
 def solution(mesh):

time: 47.1 us -> 44.9 us (0.953)
  Pallas kernels: 42 us -> 39.8 us
    pallas_call x1, Pallas kernels: 38.1 us -> 36.4 us  [sweep(): pl.pallas_call(functools.partial(sweep_kernel, edges, starts, rim), name=...]
    pallas_call x1, Pallas kernels: 3.93 us -> 3.39 us  [box_filter(): pl.pallas_call(functools.partial(box_kernel, times), name='boxes', grid=(...]
where the time goes in v3:
time: 44.9 us; the launch traced here: 44.6 us
  Pallas kernels  39.8 us (89%)
  local copies, waits for them, and re-layouts  4.76 us (11%)
    pallas_call x1, Pallas kernels, sweep(): pl.pallas_call(functools.partial(sweep_kernel, edges, starts, rim), name=...  36.4 us
    unnamed x12, local copies, waits for them, and re-layouts  4.76 us
    pallas_call x1, Pallas kernels, box_filter(): pl.pallas_call(functools.partial(box_kernel, times), name='boxes', grid=(...  3.39 us

profile of v3, /device:TPU:0, one launch (start us, length us, event | category | flops | bytes accessed | tf_op | source)
XLA Modules:
  0.0 44.6 jit_solution(2970186811649762716)
XLA Ops:
  0.0 0.0 copy-start
  0.0 1.2 %copy-done = bf16[256,2048]{1,0:T(8,128)(2,1)S(1)} copy-done((bf16[256,2048]{1,0:T(8,128)(2,1)S(1)}, bf16[256,2048]{1,0:T(8,128)(2,1)}, u32[]{:S(2)}) %copy-start) | copy-done | bytes 1048600
  1.2 0.0 copy-start.1
  1.2 0.8 %copy-done.1 = s32[256,64]{0,1:T(8,128)S(1)} copy-done((s32[256,64]{0,1:T(8,128)S(1)}, s32[256,64]{0,1:T(8,128)}, u32[]{:S(2)}) %copy-start.1) | copy-done | bytes 65560
  2.1 0.0 copy-start.2
  2.1 0.7 %copy-done.2 = s32[3,64]{1,0:T(4,128)S(1)} copy-done((s32[3,64]{1,0:T(4,128)S(1)}, s32[3,64]{1,0:T(4,128)}, u32[]{:S(2)}) %copy-start.2) | copy-done | bytes 792
  2.7 0.0 copy-start.3
  2.8 0.7 %copy-done.3 = s32[3,64]{1,0:T(4,128)S(1)} copy-done((s32[3,64]{1,0:T(4,128)S(1)}, s32[3,64]{1,0:T(4,128)}, u32[]{:S(2)}) %copy-start.3) | copy-done | bytes 792
  3.4 0.0 copy-start.4
  3.4 0.7 %copy-done.4 = s32[3,64]{1,0:T(4,128)S(1)} copy-done((s32[3,64]{1,0:T(4,128)S(1)}, s32[3,64]{1,0:T(4,128)}, u32[]{:S(2)}) %copy-start.4) | copy-done | bytes 792
  4.1 0.0 copy-start.5
  4.1 0.7 %copy-done.5 = s32[8]{0:T(128)S(1)} copy-done((s32[8]{0:T(128)S(1)}, s32[8]{0:T(128)}, u32[]{:S(2)}) %copy-start.5) | copy-done | bytes 56
  4.8 36.4 %sweep.1 = (f32[64,2176]{1,0:T(8,128)S(1)}, f32[64,128]{1,0:T(8,128)S(1)}, s32[8,128]{1,0:T(8,128)S(1)}) custom-call(bf16[256,2048]{1,0:T(8,128)(2,1)S(1)} %copy-done, s32[64,256]{1,0:T(8,128)S(1)} %bitcast.2, s32[3,64]{1,0:T(4,128)S(1)} %copy-done.2, s32[3,64]{1,0:T(4,128)S(1)} %copy-done.3, s32[3,64]{1,0:T(4,128)S(1)} %copy-done.4, s32[1,8]{1,0:T(1,128)S(1)} %bitcast.3), custom_call_target="tpu_custom_call" | custom-call | tf_op jit(solution)/shard_map/sweep/pallas_call | solution.py:331
  41.2 3.4 %boxes.1 = f32[8,64,2048]{2,1,0:T(8,128)} custom-call(s32[8,128]{1,0:T(8,128)S(1)} %get-tuple-element.8.widths_ref, f32[64,2176]{1,0:T(8,128)S(1)} %get-tuple-element.9.state_ref, f32[64,128]{1,0:T(8,128)S(1)} %get-tuple-element.10.squares_ref), custom_call_target="tpu_custom_call" | custom-call | tf_op jit(solution)/shard_map/boxes/pallas_call | solution.py:415
Async XLA Ops:
  0.0 1.2 %copy-start = (bf16[256,2048]{1,0:T(8,128)(2,1)S(1)}, bf16[256,2048]{1,0:T(8,128)(2,1)}, u32[]{:S(2)}) copy-start(bf16[256,2048]{1,0:T(8,128)(2,1)} %fb_ref.1) | copy-start | bytes 3145732
  1.2 0.8 %copy-start.1 = (s32[256,64]{0,1:T(8,128)S(1)}, s32[256,64]{0,1:T(8,128)}, u32[]{:S(2)}) copy-start(s32[256,64]{0,1:T(8,128)} %param.7) | copy-start | bytes 196612
  2.1 0.7 %copy-start.2 = (s32[3,64]{1,0:T(4,128)S(1)}, s32[3,64]{1,0:T(4,128)}, u32[]{:S(2)}) copy-start(s32[3,64]{1,0:T(4,128)} %lower_hbm.1) | copy-start | bytes 2308
  2.7 0.7 %copy-start.3 = (s32[3,64]{1,0:T(4,128)S(1)}, s32[3,64]{1,0:T(4,128)}, u32[]{:S(2)}) copy-start(s32[3,64]{1,0:T(4,128)} %upper_hbm.1) | copy-start | bytes 2308
  3.4 0.7 %copy-start.4 = (s32[3,64]{1,0:T(4,128)S(1)}, s32[3,64]{1,0:T(4,128)}, u32[]{:S(2)}) copy-start(s32[3,64]{1,0:T(4,128)} %shifts_hbm.1) | copy-start | bytes 2308
  4.1 0.7 %copy-start.5 = (s32[8]{0:T(128)S(1)}, s32[8]{0:T(128)}, u32[]{:S(2)}) copy-start(s32[8]{0:T(128)} %param.11) | copy-start | bytes 100

commit v4 on v3

--- a/solution.py
+++ b/solution.py
@@ -368,7 +368,12 @@
         compiler_params=pltpu.CompilerParams(
             collective_id=0, has_side_effects=True, vmem_limit_bytes=48 * 2**20
         ),
-    )(filterbank, delays, lower_rows, upper_rows, level_shifts, box_widths[None])
+    )(
+        *[
+            pltpu.with_memory_space_constraint(each, pltpu.HBM)
+            for each in (filterbank, delays, lower_rows, upper_rows, level_shifts, box_widths[None])
+        ]
+    )
 
 
 def box_kernel(times, widths_ref, state_ref, squares_ref, out_ref, stacked):

time: 44.9 us -> 40.2 us (0.90)
  local copies, waits for them, and re-layouts: 4.76 us -> 0 us
    unnamed x12 -> x0, local copies, waits for them, and re-layouts: 4.76 us -> none
where the time goes in v4:
time: 40.2 us; the launch traced here: 40 us
  Pallas kernels  40 us (100%)
    pallas_call x1, Pallas kernels, sweep(): pl.pallas_call(functools.partial(sweep_kernel, edges, starts, rim), name=...  36.6 us
    pallas_call x1, Pallas kernels, box_filter(): pl.pallas_call(functools.partial(box_kernel, times), name='boxes', grid=(...  3.39 us

profile of v4, /device:TPU:0, one launch (start us, length us, event | category | flops | bytes accessed | tf_op | source)
XLA Modules:
  0.0 40.0 jit_solution(18413752806646853612)
XLA Ops:
  0.0 36.6 %sweep.1 = (f32[64,2176]{1,0:T(8,128)S(1)}, f32[64,128]{1,0:T(8,128)S(1)}, s32[8,128]{1,0:T(8,128)S(1)}) custom-call(bf16[256,2048]{1,0:T(8,128)(2,1)} %fb_ref.1, s32[64,256]{1,0:T(8,128)} %bitcast.2, s32[3,64]{1,0:T(4,128)} %lower_hbm.1, s32[3,64]{1,0:T(4,128)} %upper_hbm.1, s32[3,64]{1,0:T(4,128)} %shifts_hbm.1, s32[1,8]{1,0:T(1,128)} %bitcast.3), custom_call_target="tpu_custom_call" | custom-call | tf_op jit(solution)/shard_map/sweep/pallas_call | solution.py:331
  36.6 3.4 %boxes.1 = f32[8,64,2048]{2,1,0:T(8,128)} custom-call(s32[8,128]{1,0:T(8,128)S(1)} %get-tuple-element.8.widths_ref, f32[64,2176]{1,0:T(8,128)S(1)} %get-tuple-element.9.state_ref, f32[64,128]{1,0:T(8,128)S(1)} %get-tuple-element.10.squares_ref), custom_call_target="tpu_custom_call" | custom-call | tf_op jit(solution)/shard_map/boxes/pallas_call | solution.py:420

commit v5 on v4

--- a/solution.py
+++ b/solution.py
@@ -13,6 +13,7 @@
 COARSE = DLOC // FINE
 CHUNKS = 3
 PACKED = 16
+TILES = (1024, 768, 512, 256, 128)
 MESH = pl.DeviceIdType.MESH
 
 
@@ -217,7 +218,7 @@
     def dedisperse(chunk):
         begin = skip + edges[chunk] if chunk else 0
         end = skip + edges[chunk + 1]
-        tile = 2 * LANES if (end - begin) % (2 * LANES) == 0 else LANES
+        tile = next(t for t in TILES if (end - begin) % t == 0)
 
         def step(index, carry):
             start = pl.multiple_of(begin + index * tile, LANES)
@@ -346,7 +347,7 @@
             pltpu.VMEM((1, box_widths.shape[0]), jnp.int32),
             pltpu.VMEM((channels, LANES + total), jnp.bfloat16),
             pltpu.VMEM((COARSE * rows, FINE * channels), jnp.bfloat16),
-            pltpu.VMEM((FINE * channels, 2 * LANES), jnp.bfloat16),
+            pltpu.VMEM((FINE * channels, TILES[0]), jnp.bfloat16),
             pltpu.VMEM((COARSE * rows, total), jnp.float32),
             [pltpu.VMEM((rows, width), jnp.float32) for _ in range(levels)],
             [pltpu.VMEM((rows, tail + width), jnp.float32) for _ in range(levels)],

time: 40.2 us -> 38.6 us (0.960)
  Pallas kernels: 40 us -> 38.5 us
    pallas_call x1, Pallas kernels: 36.6 us -> 35.1 us  [sweep(): pl.pallas_call(functools.partial(sweep_kernel, edges, starts, rim), name=...]
where the time goes in v5:
time: 38.6 us; the launch traced here: 38.5 us
  Pallas kernels  38.5 us (100%)
    pallas_call x1, Pallas kernels, sweep(): pl.pallas_call(functools.partial(sweep_kernel, edges, starts, rim), name=...  35.1 us
    pallas_call x1, Pallas kernels, box_filter(): pl.pallas_call(functools.partial(box_kernel, times), name='boxes', grid=(...  3.38 us

profile of v5, /device:TPU:0, one launch (start us, length us, event | category | flops | bytes accessed | tf_op | source)
XLA Modules:
  0.0 38.5 jit_solution(10284207507558522708)
XLA Ops:
  0.0 35.1 %sweep.1 = (f32[64,2176]{1,0:T(8,128)S(1)}, f32[64,128]{1,0:T(8,128)S(1)}, s32[8,128]{1,0:T(8,128)S(1)}) custom-call(bf16[256,2048]{1,0:T(8,128)(2,1)} %fb_ref.1, s32[64,256]{1,0:T(8,128)} %bitcast.2, s32[3,64]{1,0:T(4,128)} %lower_hbm.1, s32[3,64]{1,0:T(4,128)} %upper_hbm.1, s32[3,64]{1,0:T(4,128)} %shifts_hbm.1, s32[1,8]{1,0:T(1,128)} %bitcast.3), custom_call_target="tpu_custom_call" | custom-call | tf_op jit(solution)/shard_map/sweep/pallas_call | solution.py:332
  35.1 3.4 %boxes.1 = f32[8,64,2048]{2,1,0:T(8,128)} custom-call(s32[8,128]{1,0:T(8,128)S(1)} %get-tuple-element.8.widths_ref, f32[64,2176]{1,0:T(8,128)S(1)} %get-tuple-element.9.state_ref, f32[64,128]{1,0:T(8,128)S(1)} %get-tuple-element.10.squares_ref), custom_call_target="tpu_custom_call" | custom-call | tf_op jit(solution)/shard_map/boxes/pallas_call | solution.py:421
